TPU v7x, 32 devices: a whole 2x2x4 slice. The times are simulated.
32 devices in a mesh: seq: 16 (over z, x, core), fsdp: 2 (over y).
Axes of the slice: x: 2, y: 2, z: 4, core: 2. Of those that a mesh axis runs over, the one named last changes fastest.
Arguments:
- hidden: bfloat16 [2, 4096, 1024], P('fsdp', 'seq')
- w_qkv: bfloat16 [1024, 3072], P('fsdp')
- cond_vec: bfloat16 [1024], replicated, may hold values from -6 to 6
- head_w: bfloat16 [1024], replicated, may hold values from -0.1875 to 0.1875
- blocks: int32 [2, 64, 5], P('fsdp', 'seq'), may hold values from 0 to 63, as said below
- counts: int32 [2, 64], P('fsdp', 'seq'), may hold values from 1 to 4, 128 in all within a row
- time_idx: int32 [2, 4096], P('fsdp', 'seq'), may hold values from 0 to 999
- cond_mask: int32 [2, 4096], P('fsdp', 'seq'), may hold values 0 or 1
- noise: float32 [2, 4096], P('fsdp', 'seq'), may hold values from -6 to 6
Outputs:
- d_hidden: bfloat16 [2, 4096, 1024], P('fsdp', 'seq')
- grad_qkv: float32 [1024, 3072], P('fsdp')
Inputs may be any that keep to these rules, and one draw needn't show every extreme that they name: Each list holds 5 distinct blocks of its own sequence: slot 0 is the query block itself, slot 1 a block exactly 4 blocks before or after it around the cycle of 64 blocks, and the other slots blocks within 4 of it around that cycle. Each sequence's counts sum to 128.
All inputs are finite; a program needn't handle non-finite values. No bound on the sum of `counts` or of `cond_mask` on one device may be relied on, other than what follows from the above.
Results may differ from a plain program's by a relative error of at most 0.014.
Values may be sent and summed in bfloat16 or wider, within the bound.
A program may use at most 128 MiB of HBM per device.

v0:
```python
import math

import jax
import jax.numpy as jnp
from jax import lax
from jax.sharding import PartitionSpec as P

HD = 64
BLK = 64
REACH = 4
NB = 5


EPS = 1e-05


def extended_2(cells, sides, width):
    for axis, dim in sides:
        count = lax.axis_size(axis)
        head = lax.slice_in_dim(cells, 0, width, axis=dim)
        tail = lax.slice_in_dim(cells, cells.shape[dim] - width, cells.shape[dim], axis=dim)
        cells = jnp.concatenate(
            [
                lax.ppermute(tail, axis, [(i, (i + 1) % count) for i in range(count)]),
                cells,
                lax.ppermute(head, axis, [((i + 1) % count, i) for i in range(count)]),
            ],
            axis=dim,
        )
    return cells


def passed_along(value, axis, steps):
    count = lax.axis_size(axis)
    pairs = [(source, (source + steps) % count) for source in range(count)]
    return lax.ppermute(value, axis, pairs)


def time_features(steps_idx, width):
    half = width // 2
    freq = jnp.exp(-math.log(10000.0) * jnp.arange(half, dtype=jnp.float32) / half)
    angle = steps_idx.astype(jnp.float32)[:, None] * freq[None, :]
    return jnp.concatenate([jnp.sin(angle), jnp.cos(angle)], axis=1)


def body(hidden, w_qkv, cond_vec, head_w, blocks, counts, time_idx, cond_mask, noise):
    tokens = hidden.shape[1]
    width = hidden.shape[2]
    heads = width // HD
    scale = HD ** (-0.5)
    local_blocks = tokens // BLK
    ext_blocks = local_blocks + 2 * REACH
    group_heads = 4
    head_groups = heads // group_heads
    cond = cond_mask[0].astype(jnp.float32)
    head_row = head_w.astype(jnp.float32)
    h_in = (
        hidden[0].astype(jnp.float32)
        + cond[:, None] * cond_vec.astype(jnp.float32)[None, :]
        + time_features(time_idx[0], width)
    )
    inv = lax.rsqrt(jnp.mean(h_in * h_in, axis=1, keepdims=True) + EPS)
    normed = (h_in * inv).astype(jnp.bfloat16)
    columns = normed
    qkv = jnp.dot(
        columns,
        lax.all_gather(w_qkv, "fsdp", axis=0, tiled=True),
        preferred_element_type=jnp.float32,
    ).astype(jnp.bfloat16)
    query = (
        qkv[:, :width]
        .reshape(local_blocks, BLK, head_groups, group_heads, HD)
        .transpose(2, 0, 1, 3, 4)
    )
    extended = extended_2(qkv[:, width:], (("seq", 0),), REACH * BLK)
    extended = extended.reshape(ext_blocks, BLK, 2 * width)
    blocks_all = local_blocks * lax.axis_size("seq")
    first_block = lax.axis_index("seq") * local_blocks
    ext_index = jnp.remainder(blocks[0] - first_block + REACH, blocks_all)
    chosen = extended[ext_index].reshape(local_blocks, NB * BLK, 2, head_groups, group_heads, HD)
    chosen = chosen.transpose(3, 0, 1, 2, 4, 5)
    valid = lax.broadcasted_iota(jnp.int32, (local_blocks, NB), 1) <= counts[0][:, None]
    key_valid = jnp.repeat(valid, BLK, axis=1)

    def softmax_probs(group_query, keys):
        scores = (
            jnp.einsum("tqhd,tkhd->thqk", group_query, keys, preferred_element_type=jnp.float32)
            * scale
        )
        scores = jnp.where(key_valid[:, None, None, :], scores, -1e30)
        top = jnp.max(scores, axis=3, keepdims=True)
        expo = jnp.exp(scores - top)
        return expo / jnp.sum(expo, axis=3, keepdims=True)

    def forward_group(items):
        group_query, group_pairs = items
        probs = softmax_probs(group_query, group_pairs[:, :, 0])
        probs_b = probs.astype(jnp.bfloat16)
        return jnp.einsum(
            "thqk,tkhd->tqhd", probs_b, group_pairs[:, :, 1], preferred_element_type=jnp.float32
        ).astype(jnp.bfloat16)

    attn_groups = lax.map(forward_group, (query, chosen))
    attn = attn_groups.transpose(1, 2, 0, 3, 4).reshape(tokens, width)
    h_out = h_in + attn.astype(jnp.float32)
    net = jnp.sum(h_out * head_row[None, :], axis=1)
    d_net = 2.0 * (1.0 - cond) * (net + noise[0])
    d_out = d_net[:, None] * head_row[None, :]
    d_attn = (
        d_out.astype(jnp.bfloat16)
        .reshape(local_blocks, BLK, head_groups, group_heads, HD)
        .transpose(2, 0, 1, 3, 4)
    )

    def backward_group(items):
        group_query, group_pairs, group_d_attn, group_attn = items
        keys = group_pairs[:, :, 0]
        vals = group_pairs[:, :, 1]
        probs = softmax_probs(group_query, keys)
        probs_b = probs.astype(jnp.bfloat16)
        delta = jnp.sum(group_d_attn.astype(jnp.float32) * group_attn.astype(jnp.float32), axis=3)
        d_probs = jnp.einsum(
            "tqhd,tkhd->thqk", group_d_attn, vals, preferred_element_type=jnp.float32
        )
        d_scores = (probs * (d_probs - jnp.transpose(delta, (0, 2, 1))[..., None])).astype(
            jnp.bfloat16
        )
        d_query = (
            jnp.einsum("thqk,tkhd->tqhd", d_scores, keys, preferred_element_type=jnp.float32)
            * scale
        )
        d_keys = (
            jnp.einsum("thqk,tqhd->tkhd", d_scores, group_query, preferred_element_type=jnp.float32)
            * scale
        )
        d_vals = jnp.einsum(
            "thqk,tqhd->tkhd", probs_b, group_d_attn, preferred_element_type=jnp.float32
        )
        return (d_query, jnp.stack([d_keys, d_vals], axis=2))

    d_query_groups, d_pair_groups = lax.map(backward_group, (query, chosen, d_attn, attn_groups))
    d_query = d_query_groups.transpose(1, 2, 0, 3, 4).reshape(tokens, width)
    d_chosen = d_pair_groups.transpose(1, 2, 3, 0, 4, 5).reshape(local_blocks * NB, BLK, 2 * width)
    d_extended = (
        jnp.zeros((ext_blocks, BLK, 2 * width), jnp.float32).at[ext_index.reshape(-1)].add(d_chosen)
    )
    from_right = passed_along(d_extended[:REACH].astype(jnp.bfloat16), "seq", -1).astype(
        jnp.float32
    )
    from_left = passed_along(
        d_extended[ext_blocks - REACH :].astype(jnp.bfloat16), "seq", 1
    ).astype(jnp.float32)
    d_pairs = d_extended[REACH : REACH + local_blocks]
    d_pairs = d_pairs.at[:REACH].add(from_left)
    d_pairs = d_pairs.at[local_blocks - REACH :].add(from_right)
    d_qkv = jnp.concatenate([d_query, d_pairs.reshape(tokens, 2 * width)], axis=1).astype(
        jnp.bfloat16
    )
    columns = normed
    partial_grad = lax.psum_scatter(
        jnp.einsum("tc,tk->ck", columns, d_qkv, preferred_element_type=jnp.float32).astype(
            jnp.bfloat16
        ),
        "fsdp",
        scatter_dimension=0,
        tiled=True,
    )
    grad = lax.psum(partial_grad, "seq").astype(jnp.float32)
    d_normed = lax.dot_general(
        d_qkv,
        lax.all_gather(w_qkv, "fsdp", axis=0, tiled=True),
        (((1,), (1,)), ((), ())),
        preferred_element_type=jnp.float32,
    )
    d_in = inv * (d_normed - h_in * inv * inv * jnp.mean(d_normed * h_in, axis=1, keepdims=True))
    d_hidden = (d_out + d_in).astype(jnp.bfloat16)
    return (d_hidden[None], grad)


def solution(mesh):
    return jax.shard_map(
        body,
        mesh=mesh,
        in_specs=(
            P("fsdp", "seq", None),
            P("fsdp", None),
            P(),
            P(),
            P("fsdp", "seq", None),
            P("fsdp", "seq"),
            P("fsdp", "seq"),
            P("fsdp", "seq"),
            P("fsdp", "seq"),
        ),
        out_specs=(P("fsdp", "seq", None), P("fsdp", None)),
        check_vma=False,
    )
```

profile of v0, /device:TPU:0, one launch (start us, length us, event | category | flops | bytes accessed | tf_op | source)
XLA Modules:
  0.0 575.9 jit_solution(7214676377013264921)
XLA Ops:
  10.4 82.3 %all-gather.2.cloned.1.call-done = bf16[1024,3072]{1,0:T(8,128)(2,1)} async-done(((bf16[512,3072]{1,0:T(8,128)(2,1)}), bf16[1024,3072]{1,0:T(8,128)(2,1)}) %all-gather.2.cloned.1.call-update) | async-done | bytes 6291472 | tf_op jit(solution)/shard_map/all_gather | solution.py:67
  92.7 4.6 convolution_convert_fusion.2
  98.5 4.4 collective-permute-start.1
  107.7 7.9 %collective-permute-done = bf16[256,2048]{1,0:T(8,128)(2,1)} collective-permute-done((bf16[256,2048]{1,0:T(8,128)(2,1)S(1)}, bf16[256,2048]{1,0:T(8,128)(2,1)}, u32[]{:S(2)}, u32[]{:S(2)}) %collective-permute-start) | collective-permute-done | bytes 1048608 | tf_op jit(solution)/shard_map/ppermute | solution.py:24
  117.6 4.1 gather_fusion
  121.8 18.6 %reshape.286 = bf16[4,320,2,4,4,64]{5,4,3,2,1,0:T(4,128)(2,1)} reshape(bf16[20,64,2048]{2,1,0:T(8,128)(2,1)} %gather_fusion) | data formatting | bytes 10485760 | tf_op jit(solution)/shard_map/reshape | solution.py:80
  140.4 17.9 %copy.19 = bf16[4,4,320,2,4,64]{2,5,4,1,3,0:T(8,128)(2,1)} copy(bf16[4,4,320,2,4,64]{5,4,0,3,2,1:T(4,128)(2,1)} %bitcast.173) | data formatting | bytes 10485760
  158.3 26.0 %while.28 = (s32[]{:T(128)}, bf16[4,4,64,4,64]{2,4,3,1,0:T(8,128)(2,1)S(1)}, bf16[4,4,320,2,4,64]{2,5,4,1,3,0:T(8,128)(2,1)}, bf16[4,4,64,4,64]{4,2,3,1,0:T(8,128)(2,1)}, pred[4,5]{1,0:T(4,128)(4,1)S(1)}, /*index=5*/s32[]{:T(128)}) while((s32[]{:T(128)}, bf16[4,4,64,4,64]{2,4,3,1,0:T(8,128)(2,1)S(1)}, ...), condition=%wide.region_4.5_spmd.clone, body=%wide.region_1.4_spmd.clone.sunk | while | flops 128845440 | bytes 5787997 | solution.py:103
  161.7 3.0 fusion.100
  168.3 3.0 fusion.100
  174.8 3.0 fusion.100
  181.3 3.0 fusion.100
  186.9 2.5 copy.20
  194.7 67.3 %while.29 = (s32[]{:T(128)}, bf16[4,4,64,4,64]{2,4,3,1,0:T(8,128)(2,1)}, f32[4,4,320,2,4,64]{2,5,4,1,3,0:T(8,128)}, bf16[4,4,320,2,4,64]{2,5,4,1,3,0:T(8,128)(2,...) while((s32[]{:T(128)}, ...), condition=%wide.region_10.11_spmd.clone, body=%wide.region_6.10_spmd.clone.sunk | while | flops 214302016 | bytes 22319484 | solution.py:141
  196.6 2.7 fusion.109
  213.4 2.7 fusion.109
  230.2 2.7 fusion.109
  247.1 2.7 fusion.109
  262.0 23.2 %copy.24 = f32[4,320,2,4,4,64]{5,4,3,2,1,0:T(4,128)} copy(f32[4,320,2,4,4,64]{1,5,4,0,2,3:T(8,128)} %bitcast.175) | data formatting | bytes 20971520 | tf_op jit(solution)/shard_map/transpose | solution.py:143
  285.2 20.9 %reshape.306 = f32[20,64,2048]{2,1,0:T(8,128)} reshape(f32[4,320,2,4,4,64]{5,4,3,2,1,0:T(4,128)} %copy.24) | data formatting | bytes 20971520 | tf_op jit(solution)/shard_map/reshape | solution.py:143
  306.2 3.5 broadcast_in_dim.74
  309.7 22.4 %scatter_fusion = f32[12,64,2048]{2,1,0:T(8,128)} fusion(f32[12,64,2048]{2,1,0:T(8,128)} %broadcast_in_dim.74, s32[20]{0:T(128)S(1)} %fusion.68, f32[20,64,2048]{2,1,0:T(8,128)} %reshape.306), kind=kCustom, calls=%fused_computation.1 | custom fusion | flops 2621440 | bytes 31457360 | tf_op jit(solution)/shard_map/scatter-add | solution.py:145
  332.1 3.3 convert.18
  336.8 10.0 %collective-permute-start.2 = (bf16[4,64,2048]{2,1,0:T(8,128)(2,1)}, bf16[4,64,2048]{2,1,0:T(8,128)(2,1)S(1)}, u32[]{:S(2)}, u32[]{:S(2)}) collective-permute-start(bf16[4,64,2048]{2,1,0:T(8,128)(2,1)} %get-tuple-element.200), channel_id=1, source_target_pairs={{0,2},{2,4},{4,6},{6,8},{8,10},{10,12},{12,14},{14,16},{16,18},{18... | collective-permute-start | bytes 3145736 | tf_op jit(solution)/shard_map/ppermute | solution.py:36
  349.5 4.6 collective-permute-done.2
  355.1 4.4 collective-permute-done.3
  359.5 2.6 fusion.63
  362.1 4.6 convolution_convert_fusion.1
  366.8 89.6 %reduce-scatter.2.cloned.1.call-done = bf16[512,3072]{1,0:T(8,128)(2,1)} async-done(((bf16[1024,3072]{1,0:T(8,128)(2,1)}), bf16[512,3072]{1,0:T(8,128)(2,1)}) %reduce-scatter.2.cloned.1.call-update) | async-done | bytes 3145744 | tf_op jit(solution)/shard_map/reduce_scatter | solution.py:160
  456.5 4.7 multiply_reduce_fusion
  462.3 101.7 %all-reduce.2.cloned.1.call-done = bf16[512,3072]{1,0:T(8,128)(2,1)} async-done(((bf16[512,3072]{1,0:T(8,128)(2,1)}), bf16[512,3072]{1,0:T(8,128)(2,1)}) %all-reduce.2.cloned.1.call-update) | async-done | bytes 3145744 | tf_op jit(solution)/shard_map/psum | solution.py:168
  564.0 5.4 convert_element_type.117
  (140 shorter events, 95.3 us)
Async XLA Ops:
  7.2 0.8 copy-start.14
  7.2 0.8 copy-start.10
  7.2 0.8 copy-start.12
  7.2 2.8 copy-start.8
  7.2 85.5 %all-gather.2.cloned.1.call-start = ((), (), s32[]{:S(2)}) async-start(), calls=%async_computation.1 | async-start | bytes 9437184 | tf_op jit(solution)/shard_map/all_gather | solution.py:67
  7.9 448.5 %reduce-scatter.2.cloned.1.call-start = ((), (), s32[]{:S(2)}) async-start(), calls=%async_computation.2 | async-start | bytes 9437184 | tf_op jit(solution)/shard_map/reduce_scatter | solution.py:160
  10.4 87.0 %copy-start = (f32[256,1024]{1,0:T(8,128)}, f32[256,1024]{1,0:T(8,128)S(1)}, u32[]{:S(2)}) copy-start(f32[256,1024]{1,0:T(8,128)S(1)} %get-tuple-element.197) | copy-start | bytes 3145732
  97.3 1.1 copy-start.6
  97.3 5.6 copy-start.9
  97.4 5.7 copy-start.13
  97.4 6.3 %copy-start.11 = (f32[1,256]{1,0:T(1,128)S(1)}, f32[1,256]{1,0:T(1,128)}, u32[]{:S(2)}) copy-start(f32[1,256]{1,0:T(1,128)} %param.29) | copy-start | bytes 3076
  97.4 7.2 %copy-start.15 = (s32[1,4]{1,0:T(1,128)S(1)}, s32[1,4]{1,0:T(1,128)}, u32[]{:S(2)}) copy-start(s32[1,4]{1,0:T(1,128)} %param.26) | copy-start | bytes 52
  98.5 9.2 %copy-start.5 = (bf16[256,2048]{1,0:T(8,128)(2,1)}, bf16[256,2048]{1,0:T(8,128)(2,1)S(1)}, u32[]{:S(2)}) copy-start(bf16[256,2048]{1,0:T(8,128)(2,1)S(1)} %slice.82) | copy-start | bytes 3145732
  98.5 17.1 %collective-permute-start = (bf16[256,2048]{1,0:T(8,128)(2,1)S(1)}, bf16[256,2048]{1,0:T(8,128)(2,1)}, u32[]{:S(2)}, u32[]{:S(2)}) collective-permute-start(bf16[256,2048]{1,0:T(8,128)(2,1)S(1)} %slice.82), channel_id=1, source_target_pairs={{0,2},{2,4},{4,6},{6,8},{8,10},{10,12},{12,14},{14,16},{16,18},{18... | collective-permute-start | bytes 3145736 | tf_op jit(solution)/shard_map/ppermute | solution.py:24
  98.5 17.1 %collective-permute-start.1 = (bf16[256,2048]{1,0:T(8,128)(2,1)S(1)}, bf16[256,2048]{1,0:T(8,128)(2,1)}, u32[]{:S(2)}, u32[]{:S(2)}) collective-permute-start(bf16[256,2048]{1,0:T(8,128)(2,1)S(1)} %slice.82), channel_id=1, source_target_pairs={{2,0},{4,2},{6,4},{8,6},{10,8},{12,10},{14,12},{16,14},{18,16},{20... | collective-permute-start | bytes 3145736 | tf_op jit(solution)/shard_map/ppermute | solution.py:26
  140.4 17.9 %copy-start.3 = (bf16[4,4,64,4,64]{2,4,3,1,0:T(8,128)(2,1)S(1)}, bf16[4,4,64,4,64]{2,4,3,1,0:T(8,128)(2,1)}, u32[]{:S(2)}) copy-start(bf16[4,4,64,4,64]{2,4,3,1,0:T(8,128)(2,1)} %custom-call.2) | copy-start | bytes 1572868
  184.3 1.0 copy-start.4
  189.4 2.5 copy-start.1
  336.8 17.2 %collective-permute-start.2 = (bf16[4,64,2048]{2,1,0:T(8,128)(2,1)}, bf16[4,64,2048]{2,1,0:T(8,128)(2,1)S(1)}, u32[]{:S(2)}, u32[]{:S(2)}) collective-permute-start(bf16[4,64,2048]{2,1,0:T(8,128)(2,1)} %get-tuple-element.200), channel_id=1, source_target_pairs={{0,2},{2,4},{4,6},{6,8},{8,10},{10,12},{12,14},{14,16},{16,18},{18... | collective-permute-start | bytes 3145736 | tf_op jit(solution)/shard_map/ppermute | solution.py:36
  346.8 12.6 %collective-permute-start.3 = (bf16[4,64,2048]{2,1,0:T(8,128)(2,1)}, bf16[4,64,2048]{2,1,0:T(8,128)(2,1)}, u32[]{:S(2)}, u32[]{:S(2)}) collective-permute-start(bf16[4,64,2048]{2,1,0:T(8,128)(2,1)} %get-tuple-element.201), channel_id=1, source_target_pairs={{0,30},{2,0},{4,2},{6,4},{8,6},{10,8},{12,10},{14,12},{16,14},{18,... | collective-permute-start | bytes 3145736 | tf_op jit(solution)/shard_map/ppermute | solution.py:36
  349.5 12.6 %copy-start.2 = (f32[256,1024]{1,0:T(8,128)S(1)}, f32[256,1024]{1,0:T(8,128)}, u32[]{:S(2)}) copy-start(f32[256,1024]{1,0:T(8,128)} %copy-done) | copy-start | bytes 3145732
  354.1 1.0 copy-start.7
  366.8 197.2 %all-reduce.2.cloned.1.call-start = ((), (), s32[]{:S(2)}) async-start(), calls=%async_computation.3 | async-start | bytes 6291456 | tf_op jit(solution)/shard_map/psum | solution.py:168
Sparse Core Ops, SparseCore 0:
  9.6 83.0 all-gather.1
  366.9 89.5 reduce-scatter.1
  460.4 103.4 all-reduce.1
where the time goes:
time: 580 us; the launch traced here: 576 us
  waiting for transfers between devices  291 us (50%)
  local copies, waits for them, and re-layouts  130 us (22%)
  matrix products  68.9 us (12%)
  other arithmetic  56.6 us (10%)
  starting transfers between devices  14.6 us (3%)
  between operations  14 us (2%)
    psum x1, waiting for transfers between devices, body(): grad = lax.psum(partial_grad, 'seq').astype(jnp.float32)  102 us
    reduce_scatter x1, waiting for transfers between devices, body(): lax.psum_scatter(jnp.einsum('tc,tk->ck', columns, d_qkv, preferred_elemen...  89.6 us
    all_gather x1, waiting for transfers between devices, body(): lax.all_gather(w_qkv, 'fsdp', axis=0, tiled=True)  82.3 us
    transpose x1, local copies, waits for them, and re-layouts, body(): d_pair_groups.transpose(1, 2, 3, 0, 4, 5)  23.2 us
    scatter-add x1, other arithmetic, body(): jnp.zeros((ext_blocks, BLK, 2 * width), jnp.float32)  22.4 us
    unnamed x34, local copies, waits for them, and re-layouts  21.5 us
    reshape x1, local copies, waits for them, and re-layouts, body(): d_pair_groups.transpose(1, 2, 3, 0, 4, 5)  20.9 us
    reshape x1, local copies, waits for them, and re-layouts, body(): extended[ext_index]  18.6 us
  transfers between devices with their start and end apart: 7, of which 6 were waited for; matrix products, arithmetic and copies ran while one was open for 3% of the time, Pallas kernels for 0%

commit v1 on v0

v1 whole, which is shorter than its diff:
```python
import functools
import math

import jax
import jax.numpy as jnp
from jax import lax
from jax.experimental import pallas as pl
from jax.experimental.pallas import tpu as pltpu
from jax.sharding import PartitionSpec as P

HD = 64
BLK = 64
REACH = 4
NB = 5
PAIR = 2 * HD
EPS = 1e-05
SCALE = HD ** (-0.5)
NEG = -1e30
F32 = jnp.float32
BF16 = jnp.bfloat16


def shifted(value, axis, steps):
    count = lax.axis_size(axis)
    return lax.ppermute(value, axis, [(i, (i + steps) % count) for i in range(count)])


def swapped(value, bit):
    count = lax.axis_size("seq")
    return lax.ppermute(value, "seq", [(i, i ^ bit) for i in range(count)])


def two_level():
    count = lax.axis_size("seq")
    return lax.axis_size("fsdp") == 2 and count >= 4 and count & (count - 1) == 0


def gathered(shard):
    if not two_level():
        return lax.all_gather(shard, "fsdp", axis=0, tiled=True)
    rows = shard.shape[0]
    part = rows // 4
    mine = lax.axis_index("fsdp")
    place = lax.axis_index("seq") % 4
    own = lax.dynamic_slice_in_dim(shard, place * part, part, axis=0)
    first = lax.ppermute(own, "fsdp", [(0, 1), (1, 0)])
    across = swapped(first, 2)
    pieces = ((first, 0), (across, 2), (swapped(first, 1), 1), (swapped(across, 1), 3))
    full = jnp.concatenate([shard, shard], axis=0)
    for piece, bit in pieces:
        at = (1 - mine) * rows + jnp.bitwise_xor(place, bit) * part
        full = lax.dynamic_update_slice_in_dim(full, piece, at, axis=0)
    return full


def added(a, b):
    return (a.astype(F32) + b.astype(F32)).astype(BF16)


def picked(value, index, axis=0):
    return lax.dynamic_index_in_dim(value, index, axis=axis, keepdims=False)


def reduced(grad):
    if not two_level():
        piece = lax.psum_scatter(grad, "fsdp", scatter_dimension=0, tiled=True)
        return lax.psum(piece, "seq")
    count = lax.axis_size("seq")
    bits = [1 << i for i in range(count.bit_length() - 1)]
    mine = lax.axis_index("fsdp")
    seq = lax.axis_index("seq")
    rows, cols = grad.shape
    done = []
    for chunk in jnp.split(grad, 2, axis=1):
        width = chunk.shape[1]
        halves = chunk.reshape(2, 2, rows // 4, width)
        side = seq % 2
        now = added(picked(halves, side, 1), swapped(picked(halves, 1 - side, 1), 1))
        other = lax.ppermute(picked(now, 1 - mine), "fsdp", [(0, 1), (1, 0)])
        now = added(picked(now, mine), other)
        for bit in bits[1:]:
            side = (seq // bit) % 2
            halves = now.reshape(2, now.shape[0] // 2, width)
            now = added(picked(halves, side), swapped(picked(halves, 1 - side), bit))
        for bit in bits[::-1]:
            side = (seq // bit) % 2
            got = swapped(now, bit)
            low = jnp.where(side == 0, now, got)
            high = jnp.where(side == 0, got, now)
            now = jnp.concatenate([low, high], axis=0)
        done.append(now)
    return jnp.concatenate(done, axis=1)


def time_features(steps_idx, width):
    half = width // 2
    freq = jnp.exp(-math.log(10000.0) * jnp.arange(half, dtype=F32) / half)
    angle = steps_idx.astype(F32)[:, None] * freq[None, :]
    return jnp.concatenate([jnp.sin(angle), jnp.cos(angle)], axis=1)


def dot_nt(a, b):
    return lax.dot_general(a, b, (((1,), (1,)), ((), ())), preferred_element_type=F32)


def dot_nn(a, b):
    return jnp.dot(a, b, preferred_element_type=F32)


def forward_kernel(
    heads, q_ref, k_ref, v_ref, bias_ref, h_in_ref, head_ref, cond_ref, noise_ref, stats_ref, attn_ref
):
    pair = pl.program_id(0)
    lane = lax.broadcasted_iota(jnp.int32, (1, PAIR), 1)

    @pl.when(pair == 0)
    def _():
        stats_ref[...] = jnp.zeros_like(stats_ref)

    query = q_ref[...] * jnp.asarray(SCALE, BF16)
    keys = k_ref[...]
    vals = v_ref[...]
    stats = stats_ref[...]
    outs = []
    for half in range(2):
        mine = (lane < HD) if half == 0 else (lane >= HD)
        scores = dot_nt(jnp.where(mine, query, jnp.zeros_like(query)), keys) + bias_ref[...]
        top = jnp.max(scores, axis=1, keepdims=True)
        expo = jnp.exp(scores - top)
        total = jnp.sum(expo, axis=1, keepdims=True)
        probs_b = (expo * (1.0 / total)).astype(BF16)
        outs.append(dot_nn(probs_b, vals))
        stats = jnp.where(lane == 8 * pair + half, top + jnp.log(total), stats)
    stats_ref[...] = stats
    attn_ref[pair] = jnp.where(lane < HD, outs[0], outs[1]).astype(BF16)

    @pl.when(pair == pl.num_programs(0) - 1)
    def _():
        head_row = head_ref[...]
        net = jnp.zeros_like(noise_ref[...])
        for at in range(heads // 2):
            part = slice(at * PAIR, (at + 1) * PAIR)
            h_out = h_in_ref[:, part] + attn_ref[at].astype(F32)
            net = net + jnp.sum(h_out * head_row[:, part], axis=1, keepdims=True)
        d_net = 2.0 * (1.0 - cond_ref[...]) * (net + noise_ref[...])
        full = jnp.where(lane == 4, d_net, stats_ref[...])
        for at in range(heads // 2):
            part = slice(at * PAIR, (at + 1) * PAIR)
            d_attn = (d_net * head_row[:, part]).astype(BF16).astype(F32)
            prod = d_attn * attn_ref[at].astype(F32)
            low = jnp.sum(jnp.where(lane < HD, prod, 0.0), axis=1, keepdims=True)
            high = jnp.sum(jnp.where(lane < HD, 0.0, prod), axis=1, keepdims=True)
            full = jnp.where(lane == 8 * at + 2, low, full)
            full = jnp.where(lane == 8 * at + 3, high, full)
        stats_ref[...] = full


def backward_kernel(
    q_ref, k_ref, v_ref, bias_ref, bias_t_ref, stats_ref, rows_ref, d_net_ref, head_ref, d_q_ref, d_k_ref, d_v_ref
):
    pair = pl.program_id(0)
    tokens = stats_ref.shape[0]
    lane = lax.broadcasted_iota(jnp.int32, (1, PAIR), 1)
    query = q_ref[...] * jnp.asarray(SCALE, BF16)
    keys = k_ref[...]
    vals = v_ref[...]
    own_keys = k_ref[:tokens, :]
    own_vals = v_ref[:tokens, :]
    stats = stats_ref[...]
    d_attn = (d_net_ref[...] * head_ref[...]).astype(BF16)
    d_q, d_k, d_v = [], [], []
    for half in range(2):
        mine = (lane < HD) if half == 0 else (lane >= HD)
        query_m = jnp.where(mine, query, jnp.zeros_like(query))
        d_attn_m = jnp.where(mine, d_attn, jnp.zeros_like(d_attn))
        lse = jnp.sum(jnp.where(lane == 8 * pair + half, stats, 0.0), axis=1, keepdims=True)
        delta = jnp.sum(jnp.where(lane == 8 * pair + 2 + half, stats, 0.0), axis=1, keepdims=True)
        probs = jnp.exp(dot_nt(query_m[:tokens], keys) + bias_ref[...] - lse)
        d_probs = dot_nt(d_attn_m[:tokens], vals)
        d_scores = (probs * (d_probs - delta)).astype(BF16)
        d_q.append(dot_nn(d_scores, keys))
        lse_row = rows_ref[half : half + 1, :]
        delta_row = rows_ref[2 + half : 3 + half, :]
        probs_t = jnp.exp(dot_nt(own_keys, query_m) + bias_t_ref[...] - lse_row)
        d_v.append(dot_nn(probs_t.astype(BF16), d_attn))
        d_probs_t = dot_nt(own_vals, d_attn_m)
        d_scores_t = (probs_t * (d_probs_t - delta_row)).astype(BF16)
        d_k.append(dot_nn(d_scores_t, query))
    low = lane < HD
    d_q_ref[...] = (jnp.where(low, d_q[0], d_q[1]) * SCALE).astype(BF16)
    d_k_ref[...] = jnp.where(low, d_k[0], d_k[1]).astype(BF16)
    d_v_ref[...] = jnp.where(low, d_v[0], d_v[1]).astype(BF16)


def whole(shape):
    return pl.BlockSpec(shape, lambda pair: (0, 0))


def forward_call(qkv, bias, h_in, head_row, cond, noise):
    ext = qkv.shape[0]
    tokens, width = h_in.shape
    pairs = width // PAIR
    return pl.pallas_call(
        functools.partial(forward_kernel, width // HD),
        grid=(pairs,),
        in_specs=[
            pl.BlockSpec((tokens, PAIR), lambda pair: (0, pair)),
            pl.BlockSpec((ext, PAIR), lambda pair: (0, pairs + pair)),
            pl.BlockSpec((ext, PAIR), lambda pair: (0, 2 * pairs + pair)),
            whole((tokens, ext)),
            whole((tokens, width)),
            whole((1, width)),
            whole((tokens, 1)),
            whole((tokens, 1)),
        ],
        out_specs=whole((tokens, PAIR)),
        out_shape=jax.ShapeDtypeStruct((tokens, PAIR), F32),
        scratch_shapes=[pltpu.VMEM((pairs, tokens, PAIR), BF16)],
        compiler_params=pltpu.CompilerParams(vmem_limit_bytes=40 << 20),
        name="attn_forward",
    )(qkv, qkv, qkv, bias, h_in, head_row, cond, noise)


def backward_call(qkv, bias, bias_t, stats, rows, d_net, head_row):
    ext = qkv.shape[0]
    tokens = stats.shape[0]
    width = head_row.shape[1]
    pairs = width // PAIR
    return pl.pallas_call(
        backward_kernel,
        grid=(pairs,),
        in_specs=[
            pl.BlockSpec((ext, PAIR), lambda pair: (0, pair)),
            pl.BlockSpec((ext, PAIR), lambda pair: (0, pairs + pair)),
            pl.BlockSpec((ext, PAIR), lambda pair: (0, 2 * pairs + pair)),
            whole((tokens, ext)),
            whole((tokens, ext)),
            whole((tokens, PAIR)),
            pl.BlockSpec((8, ext), lambda pair: (pair, 0)),
            whole((ext, 1)),
            pl.BlockSpec((1, PAIR), lambda pair: (0, pair)),
        ],
        out_specs=[pl.BlockSpec((tokens, PAIR), lambda pair: (0, pair))] * 3,
        out_shape=[jax.ShapeDtypeStruct((tokens, width), BF16)] * 3,
        compiler_params=pltpu.CompilerParams(vmem_limit_bytes=48 << 20),
        name="attn_backward",
    )(qkv, qkv, qkv, bias, bias_t, stats, rows, d_net, head_row)


def body(hidden, w_qkv, cond_vec, head_w, blocks, counts, time_idx, cond_mask, noise):
    tokens = hidden.shape[1]
    width = hidden.shape[2]
    heads = width // HD
    local_blocks = tokens // BLK
    halo = REACH * BLK
    blocks_all = local_blocks * lax.axis_size("seq")
    first_block = lax.axis_index("seq") * local_blocks

    used = lax.broadcasted_iota(jnp.int32, (local_blocks, NB), 1) <= counts[0][:, None]
    listed = jnp.where(used, blocks[0], -1)
    listed_ext = jnp.concatenate(
        [
            listed,
            shifted(listed[local_blocks - REACH :], "seq", 1),
            shifted(listed[:REACH], "seq", -1),
        ],
        axis=0,
    )
    own_ids = first_block + jnp.arange(local_blocks, dtype=jnp.int32)
    left_ids = first_block - REACH + jnp.arange(REACH, dtype=jnp.int32)
    right_ids = first_block + local_blocks + jnp.arange(REACH, dtype=jnp.int32)
    ext_ids = jnp.remainder(jnp.concatenate([own_ids, left_ids, right_ids]), blocks_all)

    def bias_of(seen):
        seen = jnp.repeat(jnp.repeat(seen, BLK, axis=0), BLK, axis=1)
        return jnp.where(seen, 0.0, NEG).astype(F32)

    bias = bias_of(jnp.any(listed[:, None, :] == ext_ids[None, :, None], axis=2))
    bias_t = bias_of(jnp.any(listed_ext[None, :, :] == own_ids[:, None, None], axis=2))

    cond = cond_mask[0].astype(F32)[:, None]
    head_row = head_w.astype(F32)[None, :]
    h_in = (
        hidden[0].astype(F32)
        + cond * cond_vec.astype(F32)[None, :]
        + time_features(time_idx[0], width)
    )
    inv = lax.rsqrt(jnp.mean(h_in * h_in, axis=1, keepdims=True) + EPS)
    normed = (h_in * inv).astype(BF16)
    normed_ext = jnp.concatenate(
        [
            normed,
            shifted(normed[tokens - halo :], "seq", 1),
            shifted(normed[:halo], "seq", -1),
        ],
        axis=0,
    )
    weights = gathered(w_qkv)
    qkv = jnp.dot(normed_ext, weights, preferred_element_type=F32).astype(BF16)

    stats = forward_call(qkv, bias, h_in, head_row, cond, noise[0][:, None])
    rows = stats[:, : 4 * heads].T
    rows_ext = jnp.concatenate(
        [
            rows,
            shifted(rows[:, tokens - halo :], "seq", 1),
            shifted(rows[:, :halo], "seq", -1),
        ],
        axis=1,
    )
    d_net_ext = rows_ext[4][:, None]
    d_qkv = jnp.concatenate(
        backward_call(qkv, bias, bias_t, stats, rows_ext, d_net_ext, head_row), axis=1
    )

    partial_grad = jnp.einsum("tc,tk->ck", normed, d_qkv, preferred_element_type=F32).astype(BF16)
    grad = reduced(partial_grad).astype(F32)
    d_normed = lax.dot_general(
        d_qkv, weights, (((1,), (1,)), ((), ())), preferred_element_type=F32
    )
    d_out = stats[:, 4:5] * head_row
    d_in = inv * (d_normed - h_in * inv * inv * jnp.mean(d_normed * h_in, axis=1, keepdims=True))
    d_hidden = (d_out + d_in).astype(BF16)
    return (d_hidden[None], grad)


def solution(mesh):
    return jax.shard_map(
        body,
        mesh=mesh,
        in_specs=(
            P("fsdp", "seq", None),
            P("fsdp", None),
            P(),
            P(),
            P("fsdp", "seq", None),
            P("fsdp", "seq"),
            P("fsdp", "seq"),
            P("fsdp", "seq"),
            P("fsdp", "seq"),
        ),
        out_specs=(P("fsdp", "seq", None), P("fsdp", None)),
        check_vma=False,
    )
```

time: 580 us -> 223 us (0.38)
  waiting for transfers between devices: 291 us -> 105 us
  local copies, waits for them, and re-layouts: 130 us -> 15.3 us
  matrix products: 68.9 us -> 14.2 us
  Pallas kernels: 0 us -> 28.9 us
  other arithmetic: 56.6 us -> 33.8 us
  between operations: 14 us -> 1.31 us
  starting transfers between devices: 14.6 us -> 24.1 us
    psum x1 -> x0, waiting for transfers between devices: 102 us -> none  [body(): grad = lax.psum(partial_grad, 'seq').astype(jnp.float32)]
    reduce_scatter x1 -> x0, waiting for transfers between devices: 89.6 us -> none  [body(): lax.psum_scatter(jnp.einsum('tc,tk->ck', columns, d_qkv, preferred_elemen...]
    ppermute x4 -> x28, waiting for transfers between devices: 16.9 us -> 105 us  [the longest x19 63 us: swapped(): return lax.ppermute(value, 'seq', [(i, i ^ bit) for i in range(count)])]
    all_gather x1 -> x0, waiting for transfers between devices: 82.3 us -> none  [body(): lax.all_gather(w_qkv, 'fsdp', axis=0, tiled=True)]
    reshape x5 -> x0, local copies, waits for them, and re-layouts: 42.2 us -> none  [the longest x1 20.9 us: body(): d_pair_groups.transpose(1, 2, 3, 0, 4, 5)]
    dot_general x23 -> x3, matrix products: 51.7 us -> 14.2 us  [the longest x1 7.5 us: body(): qkv = jnp.dot(normed_ext, weights, preferred_element_type=F32).astype(BF16)]
    pallas_call x0 -> x2, Pallas kernels: none -> 28.9 us  [the longest x1 16.5 us: backward_call(): pl.pallas_call(backward_kernel, grid=(pairs,), in_specs=[pl.BlockSpec((ex...]
    transpose x2 -> x0, local copies, waits for them, and re-layouts: 25.2 us -> none  [the longest x1 23.2 us: body(): d_pair_groups.transpose(1, 2, 3, 0, 4, 5)]
  transfers between devices with their start and end apart: 7 -> 28, of which waited for: 6 -> 16; matrix products, arithmetic and copies ran while one was open for 3% -> 15% of each run, Pallas kernels for 0% -> 0%
where the time goes in v1:
time: 223 us
  waiting for transfers between devices  105 us (47%)
  other arithmetic  33.8 us (15%)
  Pallas kernels  28.9 us (13%)
  starting transfers between devices  24.1 us (11%)
  local copies, waits for them, and re-layouts  15.3 us (7%)
  matrix products  14.2 us (6%)
    ppermute x19, waiting for transfers between devices, swapped(): return lax.ppermute(value, 'seq', [(i, i ^ bit) for i in range(count)])  63 us
    ppermute x2, waiting for transfers between devices, reduced(): other = lax.ppermute(picked(now, 1 - mine), 'fsdp', [(0, 1), (1, 0)])  32.4 us
    pallas_call x1, Pallas kernels, backward_call(): pl.pallas_call(backward_kernel, grid=(pairs,), in_specs=[pl.BlockSpec((ex...  16.5 us
    convert_element_type x1, other arithmetic, body(): grad = reduced(partial_grad).astype(F32)  14 us
    pallas_call x1, Pallas kernels, forward_call(): pl.pallas_call(functools.partial(forward_kernel, width // HD), grid=(pair...  12.4 us
    ppermute x6, starting transfers between devices, shifted(): lax.ppermute(value, axis, [(i, (i + steps) % count) for i in range(count)])  12.1 us
    dot_general x1, matrix products, body(): qkv = jnp.dot(normed_ext, weights, preferred_element_type=F32).astype(BF16)  7.5 us
    ppermute x19, starting transfers between devices, swapped(): return lax.ppermute(value, 'seq', [(i, i ^ bit) for i in range(count)])  6.8 us
  transfers between devices with their start and end apart: 28, of which 16 were waited for; matrix products, arithmetic and copies ran while one was open for 15% of the time, Pallas kernels for 0%

profile of v1, /device:TPU:0, one launch (start us, length us, event | category | flops | bytes accessed | tf_op | source)
XLA Modules:
  0.0 222.7 jit_solution(7587150491199547869)
XLA Ops:
  1.9 3.0 %collective-permute-start.2 = (bf16[128,3072]{1,0:T(8,128)(2,1)S(1)}, bf16[128,3072]{1,0:T(8,128)(2,1)}, u32[]{:S(2)}, u32[]{:S(2)}) collective-permute-start(bf16[128,3072]{1,0:T(8,128)(2,1)S(1)} %constant_dynamic-slice_fusion), channel_id=1, source_target_pairs={{0,1},{1,0},{2,3},{3,2},{4,5},{5,4},{6,7},{7,6},{8,9},{9,8},{10,11... | collective-permute-start | bytes 2359304 | tf_op jit(solution)/shard_map/ppermute | solution.py:46
  7.0 1.9 multiply_sine_fusion
  10.5 3.7 %collective-permute-start.1 = (bf16[256,1024]{1,0:T(8,128)(2,1)S(1)}, bf16[256,1024]{1,0:T(8,128)(2,1)}, u32[]{:S(2)}, u32[]{:S(2)}) collective-permute-start(bf16[256,1024]{1,0:T(8,128)(2,1)S(1)} %multiply_convert_fusion), channel_id=1, source_target_pairs={{0,30},{2,0},{4,2},{6,4},{8,6},{10,8},{12,10},{14,12},{16,14},{18,... | collective-permute-start | bytes 1572872 | tf_op jit(solution)/shard_map/ppermute | solution.py:25
  14.3 4.4 %collective-permute-start.7 = (s32[4,5]{1,0:T(4,128)S(1)}, s32[4,5]{1,0:T(4,128)S(1)}, u32[]{:S(2)}, u32[]{:S(2)}) collective-permute-start(s32[4,5]{1,0:T(4,128)S(1)} %bitcast_select_fusion), channel_id=1, source_target_pairs={{0,30},{2,0},{4,2},{6,4},{8,6},{10,8},{12,10},{14,12},{16,14},{18,... | collective-permute-start | bytes 248 | tf_op jit(solution)/shard_map/ppermute | solution.py:25
  19.0 3.6 %collective-permute-done.2 = bf16[128,3072]{1,0:T(8,128)(2,1)} collective-permute-done((bf16[128,3072]{1,0:T(8,128)(2,1)S(1)}, bf16[128,3072]{1,0:T(8,128)(2,1)}, u32[]{:S(2)}, u32[]{:S(2)}) %collective-permute-start.2) | collective-permute-done | bytes 786464 | tf_op jit(solution)/shard_map/ppermute | solution.py:46
  25.2 6.0 %pad_maximum_fusion = bf16[1024,3072]{1,0:T(8,128)(2,1)} fusion(bf16[512,3072]{1,0:T(8,128)(2,1)} %param.10), kind=kLoop, calls=%fused_computation | loop fusion | flops 12582912 | bytes 9437184 | tf_op jit(solution)/shard_map/concatenate | solution.py:49
  31.4 11.1 %collective-permute-done.3 = bf16[128,3072]{1,0:T(8,128)(2,1)} collective-permute-done((bf16[128,3072]{1,0:T(8,128)(2,1)}, bf16[128,3072]{1,0:T(8,128)(2,1)}, u32[]{:S(2)}, u32[]{:S(2)}) %collective-permute-start.3) | collective-permute-done | bytes 786464 | tf_op jit(solution)/shard_map/ppermute | solution.py:30
  42.5 2.1 constant_dynamic-update-slice_fusion.6
  44.6 2.1 constant_dynamic-update-slice_fusion.5
  48.5 7.5 %convolution_convert_fusion.1.q_ref.k_ref.v_ref = bf16[768,3072]{1,0:T(8,128)(2,1)S(1)} fusion(bf16[1024,3072]{1,0:T(8,128)(2,1)} %constant_dynamic-update-slice_fusion.3, bf16[256,1024]{1,0:T(8,128)(2,1)} %collective-permute-done.1, bf16[256,1024]{1,0:T(8,128)(2,1)} %collective-permute-done, bf16[256,1024]{1,0:T(8,128)(2,1)S(1)} %multiply_convert_fusion), kind=kOutput, calls=%fused_computation.2 | convolution fusion | flops 4838916096 | bytes 12582912 | tf_op jit(solution)/shard_map/dot_general | solution.py:299
  56.0 12.4 %attn_forward.1.stats_ref = f32[256,128]{1,0:T(8,128)S(1)} custom-call(bf16[768,3072]{1,0:T(8,128)(2,1)S(1)} %convolution_convert_fusion.1.q_ref.k_ref.v_ref, bf16[768,3072]{1,0:T(8,128)(2,1)S(1)} %convolution_convert_fusion.1.q_ref.k_ref.v_ref, bf16[768,3072]{1,0:T(8,128)(2,1)S(1)} %convolution_convert_fusion.1.q_ref.k_ref.v_ref, ...), custom_call_target="tpu_custom_call" | custom-call | tf_op jit(solution)/shard_map/attn_forward/pallas_call | solution.py:203
  69.1 3.9 %collective-permute-start.9 = (f32[64,256]{1,0:T(8,128)}, f32[64,256]{1,0:T(8,128)}, u32[]{:S(2)}, u32[]{:S(2)}) collective-permute-start(f32[64,256]{1,0:T(8,128)} %bitcast.10), channel_id=1, source_target_pairs={{0,30},{2,0},{4,2},{6,4},{8,6},{10,8},{12,10},{14,12},{16,14},{18,... | collective-permute-start | bytes 196616 | tf_op jit(solution)/shard_map/ppermute | solution.py:25
  75.2 4.5 %collective-permute-done.8 = f32[64,256]{1,0:T(8,128)} collective-permute-done((f32[64,256]{1,0:T(8,128)}, f32[64,256]{1,0:T(8,128)}, u32[]{:S(2)}, u32[]{:S(2)}) %collective-permute-start.8) | collective-permute-done | bytes 65568 | tf_op jit(solution)/shard_map/ppermute | solution.py:25
  80.8 16.5 %attn_backward.1 = (bf16[256,1024]{1,0:T(8,128)(2,1)S(1)}, bf16[256,1024]{1,0:T(8,128)(2,1)S(1)}, bf16[256,1024]{1,0:T(8,128)(2,1)S(1)}) custom-call(bf16[768,3072]{1,0:T(8,128)(2,1)} %copy-done, bf16[768,3072]{1,0:T(8,128)(2,1)} %copy-done, bf16[768,3072]{1,0:T(8,128)(2,1)} %copy-done, f32[256,768]{1,0:T(8,128)S(1)} %copy.21.bias_ref, ...), custom_call_target="tpu_custom_call" | custom-call | tf_op jit(solution)/shard_map/attn_backward/pallas_call | solution.py:229
  98.4 1.8 convolution_convert_fusion
  102.2 1.8 dynamic-slice_bitcast_fusion.1
  104.6 4.8 %multiply_reduce_fusion = (f32[256]{0:T(256)S(1)}, f32[256,1024]{1,0:T(8,128)S(1)}) fusion(f32[256,1024]{1,0:T(8,128)S(1)} %get-tuple-element.9.h_in_ref, bf16[256,3072]{1,0:T(8,128)(2,1)S(1)} %constant_dynamic-update-slice_fusion, bf16[1024,3072]{1,0:T(8,128)(2,1)} %constant_dynamic-update-slice_fusion.3), kind=kOutput, calls=%fused_computation.22 | convolution fusion | flops 1611136768 | bytes 9962496 | tf_op jit(solution)/shard_map/dot_general | solution.py:318
  109.5 2.1 fusion
  112.9 1.9 fusion.1
  115.7 16.3 %collective-permute-done.20 = bf16[256,1536]{1,0:T(8,128)(2,1)S(1)} collective-permute-done((bf16[256,1536]{1,0:T(8,128)(2,1)S(1)}, bf16[256,1536]{1,0:T(8,128)(2,1)S(1)}, u32[]{:S(2)}, u32[]{:S(2)}) %collective-permute-start.20) | collective-permute-done | bytes 786464 | tf_op jit(solution)/shard_map/ppermute | solution.py:79
  132.3 16.1 %collective-permute-done.11 = bf16[256,1536]{1,0:T(8,128)(2,1)S(1)} collective-permute-done((bf16[256,1536]{1,0:T(8,128)(2,1)S(1)}, bf16[256,1536]{1,0:T(8,128)(2,1)S(1)}, u32[]{:S(2)}, u32[]{:S(2)}) %collective-permute-start.11) | collective-permute-done | bytes 786464 | tf_op jit(solution)/shard_map/ppermute | solution.py:79
  149.0 10.5 %collective-permute-done.12 = bf16[128,1536]{1,0:T(8,128)(2,1)S(1)} collective-permute-done((bf16[128,1536]{1,0:T(8,128)(2,1)S(1)}, bf16[128,1536]{1,0:T(8,128)(2,1)S(1)}, u32[]{:S(2)}, u32[]{:S(2)}) %collective-permute-start.12) | collective-permute-done | bytes 393248 | tf_op jit(solution)/shard_map/ppermute | solution.py:30
  159.9 7.6 %collective-permute-done.13 = bf16[64,1536]{1,0:T(8,128)(2,1)S(1)} collective-permute-done((bf16[64,1536]{1,0:T(8,128)(2,1)S(1)}, bf16[64,1536]{1,0:T(8,128)(2,1)S(1)}, u32[]{:S(2)}, u32[]{:S(2)}) %collective-permute-start.13) | collective-permute-done | bytes 196640 | tf_op jit(solution)/shard_map/ppermute | solution.py:30
  167.7 3.0 %collective-permute-start.24 = (bf16[32,1536]{1,0:T(8,128)(2,1)S(1)}, bf16[32,1536]{1,0:T(8,128)(2,1)S(1)}, u32[]{:S(2)}, u32[]{:S(2)}) collective-permute-start(bf16[32,1536]{1,0:T(8,128)(2,1)S(1)} %fusion.14), channel_id=1, source_target_pairs={{0,16},{2,18},{4,20},{6,22},{8,24},{10,26},{12,28},{14,30},{16,0},... | collective-permute-start | bytes 294920 | tf_op jit(solution)/shard_map/ppermute | solution.py:30
  170.6 5.7 %collective-permute-done.14 = bf16[32,1536]{1,0:T(8,128)(2,1)S(1)} collective-permute-done((bf16[32,1536]{1,0:T(8,128)(2,1)S(1)}, bf16[32,1536]{1,0:T(8,128)(2,1)S(1)}, u32[]{:S(2)}, u32[]{:S(2)}) %collective-permute-start.14) | collective-permute-done | bytes 98336 | tf_op jit(solution)/shard_map/ppermute | solution.py:30
  176.4 1.9 collective-permute-done.24
  178.4 3.7 %collective-permute-done.15 = bf16[32,1536]{1,0:T(8,128)(2,1)S(1)} collective-permute-done((bf16[32,1536]{1,0:T(8,128)(2,1)S(1)}, bf16[32,1536]{1,0:T(8,128)(2,1)S(1)}, u32[]{:S(2)}, u32[]{:S(2)}) %collective-permute-start.15) | collective-permute-done | bytes 98336 | tf_op jit(solution)/shard_map/ppermute | solution.py:30
  182.2 4.1 %collective-permute-done.25 = bf16[64,1536]{1,0:T(8,128)(2,1)S(1)} collective-permute-done((bf16[64,1536]{1,0:T(8,128)(2,1)S(1)}, bf16[64,1536]{1,0:T(8,128)(2,1)S(1)}, u32[]{:S(2)}, u32[]{:S(2)}) %collective-permute-start.25) | collective-permute-done | bytes 196640 | tf_op jit(solution)/shard_map/ppermute | solution.py:30
  187.1 3.3 %collective-permute-done.16 = bf16[64,1536]{1,0:T(8,128)(2,1)S(1)} collective-permute-done((bf16[64,1536]{1,0:T(8,128)(2,1)S(1)}, bf16[64,1536]{1,0:T(8,128)(2,1)S(1)}, u32[]{:S(2)}, u32[]{:S(2)}) %collective-permute-start.16) | collective-permute-done | bytes 196640 | tf_op jit(solution)/shard_map/ppermute | solution.py:30
  191.2 7.3 %collective-permute-done.26 = bf16[128,1536]{1,0:T(8,128)(2,1)S(1)} collective-permute-done((bf16[128,1536]{1,0:T(8,128)(2,1)S(1)}, bf16[128,1536]{1,0:T(8,128)(2,1)S(1)}, u32[]{:S(2)}, u32[]{:S(2)}) %collective-permute-start.26) | collective-permute-done | bytes 393248 | tf_op jit(solution)/shard_map/ppermute | solution.py:30
  198.7 7.1 %collective-permute-done.17 = bf16[128,1536]{1,0:T(8,128)(2,1)S(1)} collective-permute-done((bf16[128,1536]{1,0:T(8,128)(2,1)S(1)}, bf16[128,1536]{1,0:T(8,128)(2,1)S(1)}, u32[]{:S(2)}, u32[]{:S(2)}) %collective-permute-start.17) | collective-permute-done | bytes 393248 | tf_op jit(solution)/shard_map/ppermute | solution.py:30
  208.6 14.0 %maximum_convert_fusion = f32[512,3072]{1,0:T(8,128)} fusion(bf16[256,1536]{1,0:T(8,128)(2,1)S(1)} %get-tuple-element.15, bf16[256,1536]{1,0:T(8,128)(2,1)S(1)} %get-tuple-element.14, bf16[256,1536]{1,0:T(8,128)(2,1)S(1)} %get-tuple-element.13, bf16[256,1536]{1,0:T(8,128)(2,1)S(1)} %get-tuple-element.12), kind=kLoop, calls=%fused_computation.3 | loop fusion | flops 12582912 | bytes 9437184 | tf_op jit(solution)/shard_map/convert_element_type | solution.py:317
  (135 shorter events, 25.8 us)
Async XLA Ops:
  0.7 13.6 %copy-start.8 = (s32[1,4,5]{2,1,0:T(4,128)S(1)}, s32[1,4,5]{2,1,0:T(4,128)}, u32[]{:S(2)}) copy-start(s32[1,4,5]{2,1,0:T(4,128)} %param.13) | copy-start | bytes 244
  1.9 20.7 %collective-permute-start.2 = (bf16[128,3072]{1,0:T(8,128)(2,1)S(1)}, bf16[128,3072]{1,0:T(8,128)(2,1)}, u32[]{:S(2)}, u32[]{:S(2)}) collective-permute-start(bf16[128,3072]{1,0:T(8,128)(2,1)S(1)} %constant_dynamic-slice_fusion), channel_id=1, source_target_pairs={{0,1},{1,0},{2,3},{3,2},{4,5},{5,4},{6,7},{7,6},{8,9},{9,8},{10,11... | collective-permute-start | bytes 2359304 | tf_op jit(solution)/shard_map/ppermute | solution.py:46
  8.9 16.0 %copy-start.7 = (bf16[1024]{0:T(1024)(128)(2,1)S(1)}, bf16[1024]{0:T(1024)(128)(2,1)}, u32[]{:S(2)}) copy-start(bf16[1024]{0:T(1024)(128)(2,1)} %param.12) | copy-start | bytes 6148
  8.9 16.2 %copy-start.9 = (f32[1,256]{1,0:T(1,128)S(1)}, f32[1,256]{1,0:T(1,128)}, u32[]{:S(2)}) copy-start(f32[1,256]{1,0:T(1,128)} %param.17) | copy-start | bytes 3076
  10.4 38.0 %copy-start.5 = (bf16[256,1024]{1,0:T(8,128)(2,1)}, bf16[256,1024]{1,0:T(8,128)(2,1)S(1)}, u32[]{:S(2)}) copy-start(bf16[256,1024]{1,0:T(8,128)(2,1)S(1)} %multiply_convert_fusion) | copy-start | bytes 1572868
  10.5 38.0 %collective-permute-start.1 = (bf16[256,1024]{1,0:T(8,128)(2,1)S(1)}, bf16[256,1024]{1,0:T(8,128)(2,1)}, u32[]{:S(2)}, u32[]{:S(2)}) collective-permute-start(bf16[256,1024]{1,0:T(8,128)(2,1)S(1)} %multiply_convert_fusion), channel_id=1, source_target_pairs={{0,30},{2,0},{4,2},{6,4},{8,6},{10,8},{12,10},{14,12},{16,14},{18,... | collective-permute-start | bytes 1572872 | tf_op jit(solution)/shard_map/ppermute | solution.py:25
  14.2 34.3 %collective-permute-start = (bf16[256,1024]{1,0:T(8,128)(2,1)S(1)}, bf16[256,1024]{1,0:T(8,128)(2,1)}, u32[]{:S(2)}, u32[]{:S(2)}) collective-permute-start(bf16[256,1024]{1,0:T(8,128)(2,1)S(1)} %multiply_convert_fusion), channel_id=1, source_target_pairs={{0,2},{2,4},{4,6},{6,8},{8,10},{10,12},{12,14},{14,16},{16,18},{18... | collective-permute-start | bytes 1572872 | tf_op jit(solution)/shard_map/ppermute | solution.py:25
  14.3 16.9 %collective-permute-start.7 = (s32[4,5]{1,0:T(4,128)S(1)}, s32[4,5]{1,0:T(4,128)S(1)}, u32[]{:S(2)}, u32[]{:S(2)}) collective-permute-start(s32[4,5]{1,0:T(4,128)S(1)} %bitcast_select_fusion), channel_id=1, source_target_pairs={{0,30},{2,0},{4,2},{6,4},{8,6},{10,8},{12,10},{14,12},{16,14},{18,... | collective-permute-start | bytes 248 | tf_op jit(solution)/shard_map/ppermute | solution.py:25
  18.7 12.5 %collective-permute-start.6 = (s32[4,5]{1,0:T(4,128)S(1)}, s32[4,5]{1,0:T(4,128)S(1)}, u32[]{:S(2)}, u32[]{:S(2)}) collective-permute-start(s32[4,5]{1,0:T(4,128)S(1)} %bitcast_select_fusion), channel_id=1, source_target_pairs={{0,2},{2,4},{4,6},{6,8},{8,10},{10,12},{12,14},{14,16},{16,18},{18... | collective-permute-start | bytes 248 | tf_op jit(solution)/shard_map/ppermute | solution.py:25
  22.6 19.9 %collective-permute-start.3 = (bf16[128,3072]{1,0:T(8,128)(2,1)}, bf16[128,3072]{1,0:T(8,128)(2,1)}, u32[]{:S(2)}, u32[]{:S(2)}) collective-permute-start(bf16[128,3072]{1,0:T(8,128)(2,1)} %collective-permute-done.2), channel_id=1, source_target_pairs={{0,4},{2,6},{4,0},{6,2},{8,12},{10,14},{12,8},{14,10},{16,20},{18,... | collective-permute-start | bytes 2359304 | tf_op jit(solution)/shard_map/ppermute | solution.py:30
  31.3 15.3 %collective-permute-start.4 = (bf16[128,3072]{1,0:T(8,128)(2,1)}, bf16[128,3072]{1,0:T(8,128)(2,1)S(1)}, u32[]{:S(2)}, u32[]{:S(2)}) collective-permute-start(bf16[128,3072]{1,0:T(8,128)(2,1)} %collective-permute-done.2), channel_id=1, source_target_pairs={{0,2},{2,0},{4,6},{6,4},{8,10},{10,8},{12,14},{14,12},{16,18},{18,... | collective-permute-start | bytes 2359304 | tf_op jit(solution)/shard_map/ppermute | solution.py:30
  42.5 5.1 %collective-permute-start.5 = (bf16[128,3072]{1,0:T(8,128)(2,1)}, bf16[128,3072]{1,0:T(8,128)(2,1)S(1)}, u32[]{:S(2)}, u32[]{:S(2)}) collective-permute-start(bf16[128,3072]{1,0:T(8,128)(2,1)} %collective-permute-done.3), channel_id=1, source_target_pairs={{0,2},{2,0},{4,6},{6,4},{8,10},{10,8},{12,14},{14,12},{16,18},{18,... | collective-permute-start | bytes 2359304 | tf_op jit(solution)/shard_map/ppermute | solution.py:30
  69.1 6.1 %collective-permute-start.9 = (f32[64,256]{1,0:T(8,128)}, f32[64,256]{1,0:T(8,128)}, u32[]{:S(2)}, u32[]{:S(2)}) collective-permute-start(f32[64,256]{1,0:T(8,128)} %bitcast.10), channel_id=1, source_target_pairs={{0,30},{2,0},{4,2},{6,4},{8,6},{10,8},{12,10},{14,12},{16,14},{18,... | collective-permute-start | bytes 196616 | tf_op jit(solution)/shard_map/ppermute | solution.py:25
  73.0 6.7 %collective-permute-start.8 = (f32[64,256]{1,0:T(8,128)}, f32[64,256]{1,0:T(8,128)}, u32[]{:S(2)}, u32[]{:S(2)}) collective-permute-start(f32[64,256]{1,0:T(8,128)} %bitcast.10), channel_id=1, source_target_pairs={{0,2},{2,4},{4,6},{6,8},{8,10},{10,12},{12,14},{14,16},{16,18},{18... | collective-permute-start | bytes 196616 | tf_op jit(solution)/shard_map/ppermute | solution.py:25
  102.2 7.2 %collective-permute-start.19 = (bf16[2,256,1536]{2,1,0:T(8,128)(2,1)}, bf16[2,256,1536]{2,1,0:T(8,128)(2,1)}, u32[]{:S(2)}, u32[]{:S(2)}) collective-permute-start(bf16[2,256,1536]{2,1,0:T(8,128)(2,1)} %dynamic-slice_bitcast_fusion), channel_id=1, source_target_pairs={{0,2},{2,0},{4,6},{6,4},{8,10},{10,8},{12,14},{14,12},{16,18},{18,... | collective-permute-start | bytes 4718600 | tf_op jit(solution)/shard_map/ppermute | solution.py:30
  104.4 8.5 %collective-permute-start.10 = (bf16[2,256,1536]{2,1,0:T(8,128)(2,1)}, bf16[2,256,1536]{2,1,0:T(8,128)(2,1)}, u32[]{:S(2)}, u32[]{:S(2)}) collective-permute-start(bf16[2,256,1536]{2,1,0:T(8,128)(2,1)} %dynamic-slice_bitcast_fusion.1), channel_id=1, source_target_pairs={{0,2},{2,0},{4,6},{6,4},{8,10},{10,8},{12,14},{14,12},{16,18},{18,... | collective-permute-start | bytes 4718600 | tf_op jit(solution)/shard_map/ppermute | solution.py:30
  111.6 20.4 %collective-permute-start.20 = (bf16[256,1536]{1,0:T(8,128)(2,1)S(1)}, bf16[256,1536]{1,0:T(8,128)(2,1)S(1)}, u32[]{:S(2)}, u32[]{:S(2)}) collective-permute-start(bf16[256,1536]{1,0:T(8,128)(2,1)S(1)} %dynamic-slice_bitcast_fusion.2), channel_id=1, source_target_pairs={{0,1},{1,0},{2,3},{3,2},{4,5},{5,4},{6,7},{7,6},{8,9},{9,8},{10,11... | collective-permute-start | bytes 2359304 | tf_op jit(solution)/shard_map/ppermute | solution.py:79
  114.8 33.6 %collective-permute-start.11 = (bf16[256,1536]{1,0:T(8,128)(2,1)S(1)}, bf16[256,1536]{1,0:T(8,128)(2,1)S(1)}, u32[]{:S(2)}, u32[]{:S(2)}) collective-permute-start(bf16[256,1536]{1,0:T(8,128)(2,1)S(1)} %dynamic-slice_bitcast_fusion.3), channel_id=1, source_target_pairs={{0,1},{1,0},{2,3},{3,2},{4,5},{5,4},{6,7},{7,6},{8,9},{9,8},{10,11... | collective-permute-start | bytes 2359304 | tf_op jit(solution)/shard_map/ppermute | solution.py:79
  132.2 16.6 %collective-permute-start.21 = (bf16[128,1536]{1,0:T(8,128)(2,1)S(1)}, bf16[128,1536]{1,0:T(8,128)(2,1)S(1)}, u32[]{:S(2)}, u32[]{:S(2)}) collective-permute-start(bf16[128,1536]{1,0:T(8,128)(2,1)S(1)} %dynamic-slice_bitcast_fusion.4), channel_id=1, source_target_pairs={{0,4},{2,6},{4,0},{6,2},{8,12},{10,14},{12,8},{14,10},{16,20},{18,... | collective-permute-start | bytes 1179656 | tf_op jit(solution)/shard_map/ppermute | solution.py:30
  148.7 10.8 %collective-permute-start.12 = (bf16[128,1536]{1,0:T(8,128)(2,1)S(1)}, bf16[128,1536]{1,0:T(8,128)(2,1)S(1)}, u32[]{:S(2)}, u32[]{:S(2)}) collective-permute-start(bf16[128,1536]{1,0:T(8,128)(2,1)S(1)} %dynamic-slice_bitcast_fusion.5), channel_id=1, source_target_pairs={{0,4},{2,6},{4,0},{6,2},{8,12},{10,14},{12,8},{14,10},{16,20},{18,... | collective-permute-start | bytes 1179656 | tf_op jit(solution)/shard_map/ppermute | solution.py:30
  149.0 10.8 %collective-permute-start.22 = (bf16[64,1536]{1,0:T(8,128)(2,1)S(1)}, bf16[64,1536]{1,0:T(8,128)(2,1)S(1)}, u32[]{:S(2)}, u32[]{:S(2)}) collective-permute-start(bf16[64,1536]{1,0:T(8,128)(2,1)S(1)} %dynamic-slice_bitcast_fusion.6), channel_id=1, source_target_pairs={{0,8},{2,10},{4,12},{6,14},{8,0},{10,2},{12,4},{14,6},{16,24},{18,... | collective-permute-start | bytes 589832 | tf_op jit(solution)/shard_map/ppermute | solution.py:30
  159.7 7.8 %collective-permute-start.13 = (bf16[64,1536]{1,0:T(8,128)(2,1)S(1)}, bf16[64,1536]{1,0:T(8,128)(2,1)S(1)}, u32[]{:S(2)}, u32[]{:S(2)}) collective-permute-start(bf16[64,1536]{1,0:T(8,128)(2,1)S(1)} %dynamic-slice_bitcast_fusion.7), channel_id=1, source_target_pairs={{0,8},{2,10},{4,12},{6,14},{8,0},{10,2},{12,4},{14,6},{16,24},{18,... | collective-permute-start | bytes 589832 | tf_op jit(solution)/shard_map/ppermute | solution.py:30
  159.8 7.8 %collective-permute-start.23 = (bf16[32,1536]{1,0:T(8,128)(2,1)S(1)}, bf16[32,1536]{1,0:T(8,128)(2,1)S(1)}, u32[]{:S(2)}, u32[]{:S(2)}) collective-permute-start(bf16[32,1536]{1,0:T(8,128)(2,1)S(1)} %dynamic-slice_bitcast_fusion.8), channel_id=1, source_target_pairs={{0,16},{2,18},{4,20},{6,22},{8,24},{10,26},{12,28},{14,30},{16,0},... | collective-permute-start | bytes 294920 | tf_op jit(solution)/shard_map/ppermute | solution.py:30
  167.5 8.8 %collective-permute-start.14 = (bf16[32,1536]{1,0:T(8,128)(2,1)S(1)}, bf16[32,1536]{1,0:T(8,128)(2,1)S(1)}, u32[]{:S(2)}, u32[]{:S(2)}) collective-permute-start(bf16[32,1536]{1,0:T(8,128)(2,1)S(1)} %dynamic-slice_bitcast_fusion.9), channel_id=1, source_target_pairs={{0,16},{2,18},{4,20},{6,22},{8,24},{10,26},{12,28},{14,30},{16,0},... | collective-permute-start | bytes 294920 | tf_op jit(solution)/shard_map/ppermute | solution.py:30
  167.7 10.6 %collective-permute-start.24 = (bf16[32,1536]{1,0:T(8,128)(2,1)S(1)}, bf16[32,1536]{1,0:T(8,128)(2,1)S(1)}, u32[]{:S(2)}, u32[]{:S(2)}) collective-permute-start(bf16[32,1536]{1,0:T(8,128)(2,1)S(1)} %fusion.14), channel_id=1, source_target_pairs={{0,16},{2,18},{4,20},{6,22},{8,24},{10,26},{12,28},{14,30},{16,0},... | collective-permute-start | bytes 294920 | tf_op jit(solution)/shard_map/ppermute | solution.py:30
  176.3 5.7 %collective-permute-start.15 = (bf16[32,1536]{1,0:T(8,128)(2,1)S(1)}, bf16[32,1536]{1,0:T(8,128)(2,1)S(1)}, u32[]{:S(2)}, u32[]{:S(2)}) collective-permute-start(bf16[32,1536]{1,0:T(8,128)(2,1)S(1)} %fusion.15), channel_id=1, source_target_pairs={{0,16},{2,18},{4,20},{6,22},{8,24},{10,26},{12,28},{14,30},{16,0},... | collective-permute-start | bytes 294920 | tf_op jit(solution)/shard_map/ppermute | solution.py:30
  178.3 7.9 %collective-permute-start.25 = (bf16[64,1536]{1,0:T(8,128)(2,1)S(1)}, bf16[64,1536]{1,0:T(8,128)(2,1)S(1)}, u32[]{:S(2)}, u32[]{:S(2)}) collective-permute-start(bf16[64,1536]{1,0:T(8,128)(2,1)S(1)} %pad_maximum_fusion.7), channel_id=1, source_target_pairs={{0,8},{2,10},{4,12},{6,14},{8,0},{10,2},{12,4},{14,6},{16,24},{18,... | collective-permute-start | bytes 589832 | tf_op jit(solution)/shard_map/ppermute | solution.py:30
  182.1 8.3 %collective-permute-start.16 = (bf16[64,1536]{1,0:T(8,128)(2,1)S(1)}, bf16[64,1536]{1,0:T(8,128)(2,1)S(1)}, u32[]{:S(2)}, u32[]{:S(2)}) collective-permute-start(bf16[64,1536]{1,0:T(8,128)(2,1)S(1)} %pad_maximum_fusion.6), channel_id=1, source_target_pairs={{0,8},{2,10},{4,12},{6,14},{8,0},{10,2},{12,4},{14,6},{16,24},{18,... | collective-permute-start | bytes 589832 | tf_op jit(solution)/shard_map/ppermute | solution.py:30
  186.4 12.1 %collective-permute-start.26 = (bf16[128,1536]{1,0:T(8,128)(2,1)S(1)}, bf16[128,1536]{1,0:T(8,128)(2,1)S(1)}, u32[]{:S(2)}, u32[]{:S(2)}) collective-permute-start(bf16[128,1536]{1,0:T(8,128)(2,1)S(1)} %pad_maximum_fusion.4), channel_id=1, source_target_pairs={{0,4},{2,6},{4,0},{6,2},{8,12},{10,14},{12,8},{14,10},{16,20},{18,... | collective-permute-start | bytes 1179656 | tf_op jit(solution)/shard_map/ppermute | solution.py:30
  190.5 15.3 %collective-permute-start.17 = (bf16[128,1536]{1,0:T(8,128)(2,1)S(1)}, bf16[128,1536]{1,0:T(8,128)(2,1)S(1)}, u32[]{:S(2)}, u32[]{:S(2)}) collective-permute-start(bf16[128,1536]{1,0:T(8,128)(2,1)S(1)} %pad_maximum_fusion.3), channel_id=1, source_target_pairs={{0,4},{2,6},{4,0},{6,2},{8,12},{10,14},{12,8},{14,10},{16,20},{18,... | collective-permute-start | bytes 1179656 | tf_op jit(solution)/shard_map/ppermute | solution.py:30
  198.6 8.6 %collective-permute-start.27 = (bf16[256,1536]{1,0:T(8,128)(2,1)S(1)}, bf16[256,1536]{1,0:T(8,128)(2,1)S(1)}, u32[]{:S(2)}, u32[]{:S(2)}) collective-permute-start(bf16[256,1536]{1,0:T(8,128)(2,1)S(1)} %pad_maximum_fusion.2), channel_id=1, source_target_pairs={{0,2},{2,0},{4,6},{6,4},{8,10},{10,8},{12,14},{14,12},{16,18},{18,... | collective-permute-start | bytes 2359304 | tf_op jit(solution)/shard_map/ppermute | solution.py:30
  206.0 2.4 %collective-permute-start.18 = (bf16[256,1536]{1,0:T(8,128)(2,1)S(1)}, bf16[256,1536]{1,0:T(8,128)(2,1)S(1)}, u32[]{:S(2)}, u32[]{:S(2)}) collective-permute-start(bf16[256,1536]{1,0:T(8,128)(2,1)S(1)} %pad_maximum_fusion.1), channel_id=1, source_target_pairs={{0,2},{2,0},{4,6},{6,4},{8,10},{10,8},{12,14},{14,12},{16,18},{18,... | collective-permute-start | bytes 2359304 | tf_op jit(solution)/shard_map/ppermute | solution.py:30
  (7 other events, 42.2 us)

commit v2 on v1

--- a/solution.py
+++ b/solution.py
@@ -69,27 +69,62 @@
     bits = [1 << i for i in range(count.bit_length() - 1)]
     mine = lax.axis_index("fsdp")
     seq = lax.axis_index("seq")
-    rows, cols = grad.shape
+    rows = grad.shape[0] // 2
     done = []
-    for chunk in jnp.split(grad, 2, axis=1):
+    for at, chunk in enumerate(jnp.split(grad, 2, axis=1)):
         width = chunk.shape[1]
-        halves = chunk.reshape(2, 2, rows // 4, width)
-        side = seq % 2
-        now = added(picked(halves, side, 1), swapped(picked(halves, 1 - side, 1), 1))
-        other = lax.ppermute(picked(now, 1 - mine), "fsdp", [(0, 1), (1, 0)])
-        now = added(picked(now, mine), other)
-        for bit in bits[1:]:
+        now = chunk.reshape(2, rows, width)
+        for step, bit in enumerate(bits):
+            if step == 1 + at:
+                other = lax.ppermute(picked(now, 1 - mine), "fsdp", [(0, 1), (1, 0)])
+                now = added(picked(now, mine), other)
+            lead = now.ndim - 2
             side = (seq // bit) % 2
-            halves = now.reshape(2, now.shape[0] // 2, width)
-            now = added(picked(halves, side), swapped(picked(halves, 1 - side), bit))
-        for bit in bits[::-1]:
+            halves = now.reshape(now.shape[:lead] + (2, now.shape[lead] // 2, width))
+            sent = swapped(picked(halves, 1 - side, lead), bit)
+            now = added(picked(halves, side, lead), sent)
+        if now.ndim == 3:
+            other = lax.ppermute(picked(now, 1 - mine), "fsdp", [(0, 1), (1, 0)])
+            now = added(picked(now, mine), other)
+        for bit in bits[:0:-1]:
             side = (seq // bit) % 2
             got = swapped(now, bit)
             low = jnp.where(side == 0, now, got)
             high = jnp.where(side == 0, got, now)
             now = jnp.concatenate([low, high], axis=0)
-        done.append(now)
-    return jnp.concatenate(done, axis=1)
+        done += [now, swapped(now, 1)]
+    return joined(seq % 2, done)
+
+
+def join_kernel(side_ref, own_0, got_0, own_1, got_1, out_ref):
+    mine = pl.program_id(0) == side_ref[0]
+    width = own_0.shape[1]
+
+    @pl.when(mine)
+    def _():
+        out_ref[:, :width] = own_0[...].astype(F32)
+        out_ref[:, width:] = own_1[...].astype(F32)
+
+    @pl.when(jnp.logical_not(mine))
+    def _():
+        out_ref[:, :width] = got_0[...].astype(F32)
+        out_ref[:, width:] = got_1[...].astype(F32)
+
+
+def joined(side, parts):
+    rows, width = parts[0].shape
+    tile = min(rows, 64)
+    tiles = rows // tile
+    return pl.pallas_call(
+        join_kernel,
+        grid=(2, tiles),
+        in_specs=[pl.BlockSpec(memory_space=pltpu.SMEM)]
+        + [pl.BlockSpec((tile, width), lambda half, at: (at, 0))] * 4,
+        out_specs=pl.BlockSpec((tile, 2 * width), lambda half, at: (half * tiles + at, 0)),
+        out_shape=jax.ShapeDtypeStruct((2 * rows, 2 * width), F32),
+        compiler_params=pltpu.CompilerParams(vmem_limit_bytes=32 << 20),
+        name="join_halves",
+    )(side.astype(jnp.int32).reshape(1), *parts)
 
 
 def time_features(steps_idx, width):

time: 223 us -> 196 us (0.88)
  other arithmetic: 33.8 us -> 19.5 us
  waiting for transfers between devices: 105 us -> 94.5 us
  Pallas kernels: 28.9 us -> 32.9 us
  starting transfers between devices: 24.1 us -> 20.6 us
  matrix products: 14.2 us -> 11.3 us
    ppermute x2, waiting for transfers between devices: 32.4 us -> 17.8 us  [reduced(): other = lax.ppermute(picked(now, 1 - mine), 'fsdp', [(0, 1), (1, 0)])]
    convert_element_type x1 -> x0, other arithmetic: 14 us -> none  [body(): grad = reduced(partial_grad).astype(F32)]
    ppermute x19, waiting for transfers between devices: 63 us -> 67 us  [swapped(): return lax.ppermute(value, 'seq', [(i, i ^ bit) for i in range(count)])]
    pallas_call x0 -> x1, Pallas kernels: none -> 3.99 us  [joined(): pl.pallas_call(join_kernel, grid=(2, tiles), in_specs=[pl.BlockSpec(memor...]
    ppermute x19, starting transfers between devices: 6.8 us -> 3.61 us  [swapped(): return lax.ppermute(value, 'seq', [(i, i ^ bit) for i in range(count)])]
    dot_general x1, matrix products: 4.84 us -> 1.92 us  [body(): lax.dot_general(d_qkv, weights, (((1,), (1,)), ((), ())), preferred_eleme...]
  transfers between devices with their start and end apart: 28 -> 28, of which waited for: 16 -> 19; matrix products, arithmetic and copies ran while one was open for 15% -> 16% of each run, Pallas kernels for 0% -> 0%
where the time goes in v2:
time: 196 us; the launch traced here: 195 us
  waiting for transfers between devices  94.5 us (48%)
  Pallas kernels  32.9 us (17%)
  starting transfers between devices  20.6 us (11%)
  other arithmetic  19.5 us (10%)
  local copies, waits for them, and re-layouts  15.3 us (8%)
  matrix products  11.3 us (6%)
    ppermute x19, waiting for transfers between devices, swapped(): return lax.ppermute(value, 'seq', [(i, i ^ bit) for i in range(count)])  67 us
    ppermute x2, waiting for transfers between devices, reduced(): other = lax.ppermute(picked(now, 1 - mine), 'fsdp', [(0, 1), (1, 0)])  17.8 us
    pallas_call x1, Pallas kernels, backward_call(): pl.pallas_call(backward_kernel, grid=(pairs,), in_specs=[pl.BlockSpec((ex...  16.5 us
    pallas_call x1, Pallas kernels, forward_call(): pl.pallas_call(functools.partial(forward_kernel, width // HD), grid=(pair...  12.3 us
    ppermute x6, starting transfers between devices, shifted(): lax.ppermute(value, axis, [(i, (i + steps) % count) for i in range(count)])  12.2 us
    dot_general x1, matrix products, body(): qkv = jnp.dot(normed_ext, weights, preferred_element_type=F32).astype(BF16)  7.5 us
    ppermute x6, waiting for transfers between devices, shifted(): lax.ppermute(value, axis, [(i, (i + steps) % count) for i in range(count)])  6.1 us
    concatenate x1, other arithmetic, gathered(): full = jnp.concatenate([shard, shard], axis=0)  5.99 us
  transfers between devices with their start and end apart: 28, of which 19 were waited for; matrix products, arithmetic and copies ran while one was open for 16% of the time, Pallas kernels for 0%

profile of v2, /device:TPU:0, one launch (start us, length us, event | category | flops | bytes accessed | tf_op | source)
XLA Modules:
  0.0 195.2 jit_solution(18411441011851363249)
XLA Ops:
  1.9 3.0 %collective-permute-start.2 = (bf16[128,3072]{1,0:T(8,128)(2,1)S(1)}, bf16[128,3072]{1,0:T(8,128)(2,1)}, u32[]{:S(2)}, u32[]{:S(2)}) collective-permute-start(bf16[128,3072]{1,0:T(8,128)(2,1)S(1)} %constant_dynamic-slice_fusion), channel_id=1, source_target_pairs={{0,1},{1,0},{2,3},{3,2},{4,5},{5,4},{6,7},{7,6},{8,9},{9,8},{10,11... | collective-permute-start | bytes 2359304 | tf_op jit(solution)/shard_map/ppermute | solution.py:46
  7.0 1.9 multiply_sine_fusion
  10.5 3.7 %collective-permute-start.1 = (bf16[256,1024]{1,0:T(8,128)(2,1)S(1)}, bf16[256,1024]{1,0:T(8,128)(2,1)}, u32[]{:S(2)}, u32[]{:S(2)}) collective-permute-start(bf16[256,1024]{1,0:T(8,128)(2,1)S(1)} %multiply_convert_fusion), channel_id=1, source_target_pairs={{0,30},{2,0},{4,2},{6,4},{8,6},{10,8},{12,10},{14,12},{16,14},{18,... | collective-permute-start | bytes 1572872 | tf_op jit(solution)/shard_map/ppermute | solution.py:25
  14.3 4.4 %collective-permute-start.7 = (s32[4,5]{1,0:T(4,128)S(1)}, s32[4,5]{1,0:T(4,128)S(1)}, u32[]{:S(2)}, u32[]{:S(2)}) collective-permute-start(s32[4,5]{1,0:T(4,128)S(1)} %bitcast_select_fusion), channel_id=1, source_target_pairs={{0,30},{2,0},{4,2},{6,4},{8,6},{10,8},{12,10},{14,12},{16,14},{18,... | collective-permute-start | bytes 248 | tf_op jit(solution)/shard_map/ppermute | solution.py:25
  19.0 3.6 %collective-permute-done.2 = bf16[128,3072]{1,0:T(8,128)(2,1)} collective-permute-done((bf16[128,3072]{1,0:T(8,128)(2,1)S(1)}, bf16[128,3072]{1,0:T(8,128)(2,1)}, u32[]{:S(2)}, u32[]{:S(2)}) %collective-permute-start.2) | collective-permute-done | bytes 786464 | tf_op jit(solution)/shard_map/ppermute | solution.py:46
  25.2 6.0 %pad_maximum_fusion = bf16[1024,3072]{1,0:T(8,128)(2,1)} fusion(bf16[512,3072]{1,0:T(8,128)(2,1)} %param.10), kind=kLoop, calls=%fused_computation | loop fusion | flops 12582912 | bytes 9437184 | tf_op jit(solution)/shard_map/concatenate | solution.py:49
  31.4 11.1 %collective-permute-done.3 = bf16[128,3072]{1,0:T(8,128)(2,1)} collective-permute-done((bf16[128,3072]{1,0:T(8,128)(2,1)}, bf16[128,3072]{1,0:T(8,128)(2,1)}, u32[]{:S(2)}, u32[]{:S(2)}) %collective-permute-start.3) | collective-permute-done | bytes 786464 | tf_op jit(solution)/shard_map/ppermute | solution.py:30
  42.5 2.1 %constant_dynamic-update-slice_fusion.6 = bf16[1024,3072]{1,0:T(8,128)(2,1)} fusion(bf16[1024,3072]{1,0:T(8,128)(2,1)} %pad_maximum_fusion, bf16[128,3072]{1,0:T(8,128)(2,1)} %collective-permute-done.2, s32[]{:T(128)S(6)} %select_n.222), kind=kLoop, calls=%fused_computation.76 | loop fusion | bytes 1572868 | tf_op jit(solution)/shard_map/dynamic_update_slice | solution.py:52
  44.6 2.1 %constant_dynamic-update-slice_fusion.5 = bf16[1024,3072]{1,0:T(8,128)(2,1)} fusion(bf16[1024,3072]{1,0:T(8,128)(2,1)} %constant_dynamic-update-slice_fusion.6, bf16[128,3072]{1,0:T(8,128)(2,1)} %collective-permute-done.3, s32[]{:T(128)S(6)} %select_n.223), kind=kLoop, calls=%fused_computation.75 | loop fusion | bytes 1572868 | tf_op jit(solution)/shard_map/dynamic_update_slice | solution.py:52
  48.5 7.5 %convolution_convert_fusion.1.q_ref.k_ref.v_ref = bf16[768,3072]{1,0:T(8,128)(2,1)S(1)} fusion(bf16[1024,3072]{1,0:T(8,128)(2,1)} %constant_dynamic-update-slice_fusion.3, bf16[256,1024]{1,0:T(8,128)(2,1)} %collective-permute-done.1, bf16[256,1024]{1,0:T(8,128)(2,1)} %collective-permute-done, bf16[256,1024]{1,0:T(8,128)(2,1)S(1)} %multiply_convert_fusion), kind=kOutput, calls=%fused_computation.2 | convolution fusion | flops 4838916096 | bytes 12582912 | tf_op jit(solution)/shard_map/dot_general | solution.py:334
  56.0 12.3 %attn_forward.1.stats_ref = f32[256,128]{1,0:T(8,128)S(1)} custom-call(bf16[768,3072]{1,0:T(8,128)(2,1)S(1)} %convolution_convert_fusion.1.q_ref.k_ref.v_ref, bf16[768,3072]{1,0:T(8,128)(2,1)S(1)} %convolution_convert_fusion.1.q_ref.k_ref.v_ref, bf16[768,3072]{1,0:T(8,128)(2,1)S(1)} %convolution_convert_fusion.1.q_ref.k_ref.v_ref, ...), custom_call_target="tpu_custom_call" | custom-call | tf_op jit(solution)/shard_map/attn_forward/pallas_call | solution.py:238
  69.1 4.0 %collective-permute-start.9 = (f32[64,256]{1,0:T(8,128)}, f32[64,256]{1,0:T(8,128)}, u32[]{:S(2)}, u32[]{:S(2)}) collective-permute-start(f32[64,256]{1,0:T(8,128)} %bitcast.10), channel_id=1, source_target_pairs={{0,30},{2,0},{4,2},{6,4},{8,6},{10,8},{12,10},{14,12},{16,14},{18,... | collective-permute-start | bytes 196616 | tf_op jit(solution)/shard_map/ppermute | solution.py:25
  75.3 4.5 %collective-permute-done.8 = f32[64,256]{1,0:T(8,128)} collective-permute-done((f32[64,256]{1,0:T(8,128)}, f32[64,256]{1,0:T(8,128)}, u32[]{:S(2)}, u32[]{:S(2)}) %collective-permute-start.8) | collective-permute-done | bytes 65568 | tf_op jit(solution)/shard_map/ppermute | solution.py:25
  80.9 16.5 %attn_backward.1 = (bf16[256,1024]{1,0:T(8,128)(2,1)S(1)}, bf16[256,1024]{1,0:T(8,128)(2,1)S(1)}, bf16[256,1024]{1,0:T(8,128)(2,1)S(1)}) custom-call(bf16[768,3072]{1,0:T(8,128)(2,1)} %copy-done, bf16[768,3072]{1,0:T(8,128)(2,1)} %copy-done, bf16[768,3072]{1,0:T(8,128)(2,1)} %copy-done, f32[256,768]{1,0:T(8,128)S(1)} %copy.23.bias_ref, ...), custom_call_target="tpu_custom_call" | custom-call | tf_op jit(solution)/shard_map/attn_backward/pallas_call | solution.py:264
  98.5 1.8 convolution_convert_fusion
  102.3 1.8 dynamic-slice_bitcast_fusion
  106.0 2.3 %fusion.1 = bf16[2,256,1536]{2,1,0:T(8,128)(2,1)S(1)} fusion(bf16[2,256,1536]{2,1,0:T(8,128)(2,1)} %collective-permute-done.10, bf16[2,2,256,1536]{3,2,1,0:T(8,128)(2,1)} %bitcast.97, s32[]{:T(128)S(6)} %select_n.244), kind=kLoop, calls=%fused_computation.6 | loop fusion | flops 3145728 | bytes 4718596 | tf_op jit(solution)/shard_map/convert_element_type | solution.py:57
  109.7 1.9 fusion
  111.9 16.1 %collective-permute-done.11 = bf16[256,1536]{1,0:T(8,128)(2,1)S(1)} collective-permute-done((bf16[256,1536]{1,0:T(8,128)(2,1)S(1)}, bf16[256,1536]{1,0:T(8,128)(2,1)S(1)}, u32[]{:S(2)}, u32[]{:S(2)}) %collective-permute-start.11) | collective-permute-done | bytes 786464 | tf_op jit(solution)/shard_map/ppermute | solution.py:79
  128.4 3.3 %collective-permute-done.20 = bf16[2,128,1536]{2,1,0:T(8,128)(2,1)S(1)} collective-permute-done((bf16[2,128,1536]{2,1,0:T(8,128)(2,1)S(1)}, bf16[2,128,1536]{2,1,0:T(8,128)(2,1)S(1)}, u32[]{:S(2)}, u32[]{:S(2)}) %collective-permute-start.20) | collective-permute-done | bytes 786464 | tf_op jit(solution)/shard_map/ppermute | solution.py:30
  132.4 7.0 %collective-permute-done.12 = bf16[128,1536]{1,0:T(8,128)(2,1)S(1)} collective-permute-done((bf16[128,1536]{1,0:T(8,128)(2,1)S(1)}, bf16[128,1536]{1,0:T(8,128)(2,1)S(1)}, u32[]{:S(2)}, u32[]{:S(2)}) %collective-permute-start.12) | collective-permute-done | bytes 393248 | tf_op jit(solution)/shard_map/ppermute | solution.py:30
  141.9 5.6 %collective-permute-done.13 = bf16[64,1536]{1,0:T(8,128)(2,1)S(1)} collective-permute-done((bf16[64,1536]{1,0:T(8,128)(2,1)S(1)}, bf16[64,1536]{1,0:T(8,128)(2,1)S(1)}, u32[]{:S(2)}, u32[]{:S(2)}) %collective-permute-start.13) | collective-permute-done | bytes 196640 | tf_op jit(solution)/shard_map/ppermute | solution.py:30
  147.7 3.2 %collective-permute-done.22 = bf16[64,1536]{1,0:T(8,128)(2,1)S(1)} collective-permute-done((bf16[64,1536]{1,0:T(8,128)(2,1)S(1)}, bf16[64,1536]{1,0:T(8,128)(2,1)S(1)}, u32[]{:S(2)}, u32[]{:S(2)}) %collective-permute-start.22) | collective-permute-done | bytes 196640 | tf_op jit(solution)/shard_map/ppermute | solution.py:30
  151.0 6.9 %collective-permute-done.14 = bf16[32,1536]{1,0:T(8,128)(2,1)S(1)} collective-permute-done((bf16[32,1536]{1,0:T(8,128)(2,1)S(1)}, bf16[32,1536]{1,0:T(8,128)(2,1)S(1)}, u32[]{:S(2)}, u32[]{:S(2)}) %collective-permute-start.14) | collective-permute-done | bytes 98336 | tf_op jit(solution)/shard_map/ppermute | solution.py:30
  158.0 4.1 %collective-permute-done.23 = bf16[32,1536]{1,0:T(8,128)(2,1)S(1)} collective-permute-done((bf16[32,1536]{1,0:T(8,128)(2,1)S(1)}, bf16[32,1536]{1,0:T(8,128)(2,1)S(1)}, u32[]{:S(2)}, u32[]{:S(2)}) %collective-permute-start.23) | collective-permute-done | bytes 98336 | tf_op jit(solution)/shard_map/ppermute | solution.py:30
  162.2 3.1 %collective-permute-done.15 = bf16[32,1536]{1,0:T(8,128)(2,1)S(1)} collective-permute-done((bf16[32,1536]{1,0:T(8,128)(2,1)S(1)}, bf16[32,1536]{1,0:T(8,128)(2,1)S(1)}, u32[]{:S(2)}, u32[]{:S(2)}) %collective-permute-start.15) | collective-permute-done | bytes 98336 | tf_op jit(solution)/shard_map/ppermute | solution.py:30
  165.4 2.4 %collective-permute-done.24 = bf16[32,1536]{1,0:T(8,128)(2,1)S(1)} collective-permute-done((bf16[32,1536]{1,0:T(8,128)(2,1)S(1)}, bf16[32,1536]{1,0:T(8,128)(2,1)S(1)}, u32[]{:S(2)}, u32[]{:S(2)}) %collective-permute-start.24) | collective-permute-done | bytes 98336 | tf_op jit(solution)/shard_map/ppermute | solution.py:30
  167.9 4.7 %collective-permute-done.16 = bf16[64,1536]{1,0:T(8,128)(2,1)S(1)} collective-permute-done((bf16[64,1536]{1,0:T(8,128)(2,1)S(1)}, bf16[64,1536]{1,0:T(8,128)(2,1)S(1)}, u32[]{:S(2)}, u32[]{:S(2)}) %collective-permute-start.16) | collective-permute-done | bytes 196640 | tf_op jit(solution)/shard_map/ppermute | solution.py:30
  175.2 8.5 %collective-permute-done.17 = bf16[128,1536]{1,0:T(8,128)(2,1)S(1)} collective-permute-done((bf16[128,1536]{1,0:T(8,128)(2,1)S(1)}, bf16[128,1536]{1,0:T(8,128)(2,1)S(1)}, u32[]{:S(2)}, u32[]{:S(2)}) %collective-permute-start.17) | collective-permute-done | bytes 393248 | tf_op jit(solution)/shard_map/ppermute | solution.py:30
  183.9 3.9 %collective-permute-done.26 = bf16[128,1536]{1,0:T(8,128)(2,1)S(1)} collective-permute-done((bf16[128,1536]{1,0:T(8,128)(2,1)S(1)}, bf16[128,1536]{1,0:T(8,128)(2,1)S(1)}, u32[]{:S(2)}, u32[]{:S(2)}) %collective-permute-start.26) | collective-permute-done | bytes 393248 | tf_op jit(solution)/shard_map/ppermute | solution.py:30
  188.1 1.9 multiply_reduce_fusion
  191.2 4.0 %join_halves.1 = f32[512,3072]{1,0:T(8,128)} custom-call(s32[1]{0:T(128)} %bitcast.13.side_ref, bf16[256,1536]{1,0:T(8,128)(2,1)S(1)} %pad_maximum_fusion.1.own_0, bf16[256,1536]{1,0:T(8,128)(2,1)S(1)} %collective-permute-done.18.got_0, bf16[256,1536]{1,0:T(8,128)(2,1)S(1)} %pad_maximum_fusion.2.own_1, bf16[256,1536]{1,0:T(8,128)(2,1)S(1)} %collective-permute-done.27.got_1), custom_call_target="tpu_custom_call" | custom-call | tf_op jit(solution)/shard_map/join_halves/pallas_call | solution.py:118
  (136 shorter events, 28.7 us)
Async XLA Ops:
  1.9 20.7 %collective-permute-start.2 = (bf16[128,3072]{1,0:T(8,128)(2,1)S(1)}, bf16[128,3072]{1,0:T(8,128)(2,1)}, u32[]{:S(2)}, u32[]{:S(2)}) collective-permute-start(bf16[128,3072]{1,0:T(8,128)(2,1)S(1)} %constant_dynamic-slice_fusion), channel_id=1, source_target_pairs={{0,1},{1,0},{2,3},{3,2},{4,5},{5,4},{6,7},{7,6},{8,9},{9,8},{10,11... | collective-permute-start | bytes 2359304 | tf_op jit(solution)/shard_map/ppermute | solution.py:46
  8.9 16.0 %copy-start.6 = (bf16[1024]{0:T(1024)(128)(2,1)S(1)}, bf16[1024]{0:T(1024)(128)(2,1)}, u32[]{:S(2)}) copy-start(bf16[1024]{0:T(1024)(128)(2,1)} %param.12) | copy-start | bytes 6148
  8.9 16.2 %copy-start.8 = (f32[1,256]{1,0:T(1,128)S(1)}, f32[1,256]{1,0:T(1,128)}, u32[]{:S(2)}) copy-start(f32[1,256]{1,0:T(1,128)} %param.17) | copy-start | bytes 3076
  10.5 38.0 %copy-start.4 = (bf16[256,1024]{1,0:T(8,128)(2,1)}, bf16[256,1024]{1,0:T(8,128)(2,1)S(1)}, u32[]{:S(2)}) copy-start(bf16[256,1024]{1,0:T(8,128)(2,1)S(1)} %multiply_convert_fusion) | copy-start | bytes 1572868
  10.5 38.0 %collective-permute-start.1 = (bf16[256,1024]{1,0:T(8,128)(2,1)S(1)}, bf16[256,1024]{1,0:T(8,128)(2,1)}, u32[]{:S(2)}, u32[]{:S(2)}) collective-permute-start(bf16[256,1024]{1,0:T(8,128)(2,1)S(1)} %multiply_convert_fusion), channel_id=1, source_target_pairs={{0,30},{2,0},{4,2},{6,4},{8,6},{10,8},{12,10},{14,12},{16,14},{18,... | collective-permute-start | bytes 1572872 | tf_op jit(solution)/shard_map/ppermute | solution.py:25
  14.2 34.3 %collective-permute-start = (bf16[256,1024]{1,0:T(8,128)(2,1)S(1)}, bf16[256,1024]{1,0:T(8,128)(2,1)}, u32[]{:S(2)}, u32[]{:S(2)}) collective-permute-start(bf16[256,1024]{1,0:T(8,128)(2,1)S(1)} %multiply_convert_fusion), channel_id=1, source_target_pairs={{0,2},{2,4},{4,6},{6,8},{8,10},{10,12},{12,14},{14,16},{16,18},{18... | collective-permute-start | bytes 1572872 | tf_op jit(solution)/shard_map/ppermute | solution.py:25
  14.3 16.9 %collective-permute-start.7 = (s32[4,5]{1,0:T(4,128)S(1)}, s32[4,5]{1,0:T(4,128)S(1)}, u32[]{:S(2)}, u32[]{:S(2)}) collective-permute-start(s32[4,5]{1,0:T(4,128)S(1)} %bitcast_select_fusion), channel_id=1, source_target_pairs={{0,30},{2,0},{4,2},{6,4},{8,6},{10,8},{12,10},{14,12},{16,14},{18,... | collective-permute-start | bytes 248 | tf_op jit(solution)/shard_map/ppermute | solution.py:25
  18.7 12.5 %collective-permute-start.6 = (s32[4,5]{1,0:T(4,128)S(1)}, s32[4,5]{1,0:T(4,128)S(1)}, u32[]{:S(2)}, u32[]{:S(2)}) collective-permute-start(s32[4,5]{1,0:T(4,128)S(1)} %bitcast_select_fusion), channel_id=1, source_target_pairs={{0,2},{2,4},{4,6},{6,8},{8,10},{10,12},{12,14},{14,16},{16,18},{18... | collective-permute-start | bytes 248 | tf_op jit(solution)/shard_map/ppermute | solution.py:25
  22.6 19.9 %collective-permute-start.3 = (bf16[128,3072]{1,0:T(8,128)(2,1)}, bf16[128,3072]{1,0:T(8,128)(2,1)}, u32[]{:S(2)}, u32[]{:S(2)}) collective-permute-start(bf16[128,3072]{1,0:T(8,128)(2,1)} %collective-permute-done.2), channel_id=1, source_target_pairs={{0,4},{2,6},{4,0},{6,2},{8,12},{10,14},{12,8},{14,10},{16,20},{18,... | collective-permute-start | bytes 2359304 | tf_op jit(solution)/shard_map/ppermute | solution.py:30
  31.3 15.3 %collective-permute-start.4 = (bf16[128,3072]{1,0:T(8,128)(2,1)}, bf16[128,3072]{1,0:T(8,128)(2,1)S(1)}, u32[]{:S(2)}, u32[]{:S(2)}) collective-permute-start(bf16[128,3072]{1,0:T(8,128)(2,1)} %collective-permute-done.2), channel_id=1, source_target_pairs={{0,2},{2,0},{4,6},{6,4},{8,10},{10,8},{12,14},{14,12},{16,18},{18,... | collective-permute-start | bytes 2359304 | tf_op jit(solution)/shard_map/ppermute | solution.py:30
  42.5 5.1 %collective-permute-start.5 = (bf16[128,3072]{1,0:T(8,128)(2,1)}, bf16[128,3072]{1,0:T(8,128)(2,1)S(1)}, u32[]{:S(2)}, u32[]{:S(2)}) collective-permute-start(bf16[128,3072]{1,0:T(8,128)(2,1)} %collective-permute-done.3), channel_id=1, source_target_pairs={{0,2},{2,0},{4,6},{6,4},{8,10},{10,8},{12,14},{14,12},{16,18},{18,... | collective-permute-start | bytes 2359304 | tf_op jit(solution)/shard_map/ppermute | solution.py:30
  69.1 6.2 %collective-permute-start.9 = (f32[64,256]{1,0:T(8,128)}, f32[64,256]{1,0:T(8,128)}, u32[]{:S(2)}, u32[]{:S(2)}) collective-permute-start(f32[64,256]{1,0:T(8,128)} %bitcast.10), channel_id=1, source_target_pairs={{0,30},{2,0},{4,2},{6,4},{8,6},{10,8},{12,10},{14,12},{16,14},{18,... | collective-permute-start | bytes 196616 | tf_op jit(solution)/shard_map/ppermute | solution.py:25
  73.0 6.7 %collective-permute-start.8 = (f32[64,256]{1,0:T(8,128)}, f32[64,256]{1,0:T(8,128)}, u32[]{:S(2)}, u32[]{:S(2)}) collective-permute-start(f32[64,256]{1,0:T(8,128)} %bitcast.10), channel_id=1, source_target_pairs={{0,2},{2,4},{4,6},{6,8},{8,10},{10,12},{12,14},{14,16},{16,18},{18... | collective-permute-start | bytes 196616 | tf_op jit(solution)/shard_map/ppermute | solution.py:25
  102.3 3.8 %collective-permute-start.10 = (bf16[2,256,1536]{2,1,0:T(8,128)(2,1)}, bf16[2,256,1536]{2,1,0:T(8,128)(2,1)}, u32[]{:S(2)}, u32[]{:S(2)}) collective-permute-start(bf16[2,256,1536]{2,1,0:T(8,128)(2,1)} %dynamic-slice_bitcast_fusion.1), channel_id=1, source_target_pairs={{0,2},{2,0},{4,6},{6,4},{8,10},{10,8},{12,14},{14,12},{16,18},{18,... | collective-permute-start | bytes 4718600 | tf_op jit(solution)/shard_map/ppermute | solution.py:30
  104.4 5.2 %collective-permute-start.19 = (bf16[2,256,1536]{2,1,0:T(8,128)(2,1)}, bf16[2,256,1536]{2,1,0:T(8,128)(2,1)}, u32[]{:S(2)}, u32[]{:S(2)}) collective-permute-start(bf16[2,256,1536]{2,1,0:T(8,128)(2,1)} %dynamic-slice_bitcast_fusion), channel_id=1, source_target_pairs={{0,2},{2,0},{4,6},{6,4},{8,10},{10,8},{12,14},{14,12},{16,18},{18,... | collective-permute-start | bytes 4718600 | tf_op jit(solution)/shard_map/ppermute | solution.py:30
  108.4 19.6 %collective-permute-start.11 = (bf16[256,1536]{1,0:T(8,128)(2,1)S(1)}, bf16[256,1536]{1,0:T(8,128)(2,1)S(1)}, u32[]{:S(2)}, u32[]{:S(2)}) collective-permute-start(bf16[256,1536]{1,0:T(8,128)(2,1)S(1)} %dynamic-slice_bitcast_fusion.3), channel_id=1, source_target_pairs={{0,1},{1,0},{2,3},{3,2},{4,5},{5,4},{6,7},{7,6},{8,9},{9,8},{10,11... | collective-permute-start | bytes 2359304 | tf_op jit(solution)/shard_map/ppermute | solution.py:79
  111.6 20.1 %collective-permute-start.20 = (bf16[2,128,1536]{2,1,0:T(8,128)(2,1)S(1)}, bf16[2,128,1536]{2,1,0:T(8,128)(2,1)S(1)}, u32[]{:S(2)}, u32[]{:S(2)}) collective-permute-start(bf16[2,128,1536]{2,1,0:T(8,128)(2,1)S(1)} %dynamic-slice_bitcast_fusion.2), channel_id=1, source_target_pairs={{0,4},{2,6},{4,0},{6,2},{8,12},{10,14},{12,8},{14,10},{16,20},{18,... | collective-permute-start | bytes 2359304 | tf_op jit(solution)/shard_map/ppermute | solution.py:30
  128.3 11.1 %collective-permute-start.12 = (bf16[128,1536]{1,0:T(8,128)(2,1)S(1)}, bf16[128,1536]{1,0:T(8,128)(2,1)S(1)}, u32[]{:S(2)}, u32[]{:S(2)}) collective-permute-start(bf16[128,1536]{1,0:T(8,128)(2,1)S(1)} %dynamic-slice_bitcast_fusion.5), channel_id=1, source_target_pairs={{0,4},{2,6},{4,0},{6,2},{8,12},{10,14},{12,8},{14,10},{16,20},{18,... | collective-permute-start | bytes 1179656 | tf_op jit(solution)/shard_map/ppermute | solution.py:30
  131.9 9.4 %collective-permute-start.21 = (bf16[128,1536]{1,0:T(8,128)(2,1)S(1)}, bf16[128,1536]{1,0:T(8,128)(2,1)S(1)}, u32[]{:S(2)}, u32[]{:S(2)}) collective-permute-start(bf16[128,1536]{1,0:T(8,128)(2,1)S(1)} %dynamic-slice_bitcast_fusion.4), channel_id=1, source_target_pairs={{0,1},{1,0},{2,3},{3,2},{4,5},{5,4},{6,7},{7,6},{8,9},{9,8},{10,11... | collective-permute-start | bytes 1179656 | tf_op jit(solution)/shard_map/ppermute | solution.py:79
  139.6 7.9 %collective-permute-start.13 = (bf16[64,1536]{1,0:T(8,128)(2,1)S(1)}, bf16[64,1536]{1,0:T(8,128)(2,1)S(1)}, u32[]{:S(2)}, u32[]{:S(2)}) collective-permute-start(bf16[64,1536]{1,0:T(8,128)(2,1)S(1)} %dynamic-slice_bitcast_fusion.7), channel_id=1, source_target_pairs={{0,8},{2,10},{4,12},{6,14},{8,0},{10,2},{12,4},{14,6},{16,24},{18,... | collective-permute-start | bytes 589832 | tf_op jit(solution)/shard_map/ppermute | solution.py:30
  141.3 46.8 %slice-start = ((s8[6291456]{0:T(1024)(128)(4,1)}), s8[4194304]{0:T(1024)(128)(4,1)S(1)}, s32[]{:S(2)}) async-start(s8[6291456]{0:T(1024)(128)(4,1)} %bitcast.100), calls=%async_computation | async-start | bytes 8388608
  141.4 9.4 %collective-permute-start.22 = (bf16[64,1536]{1,0:T(8,128)(2,1)S(1)}, bf16[64,1536]{1,0:T(8,128)(2,1)S(1)}, u32[]{:S(2)}, u32[]{:S(2)}) collective-permute-start(bf16[64,1536]{1,0:T(8,128)(2,1)S(1)} %dynamic-slice_bitcast_fusion.6), channel_id=1, source_target_pairs={{0,8},{2,10},{4,12},{6,14},{8,0},{10,2},{12,4},{14,6},{16,24},{18,... | collective-permute-start | bytes 589832 | tf_op jit(solution)/shard_map/ppermute | solution.py:30
  147.6 10.3 %collective-permute-start.14 = (bf16[32,1536]{1,0:T(8,128)(2,1)S(1)}, bf16[32,1536]{1,0:T(8,128)(2,1)S(1)}, u32[]{:S(2)}, u32[]{:S(2)}) collective-permute-start(bf16[32,1536]{1,0:T(8,128)(2,1)S(1)} %dynamic-slice_bitcast_fusion.9), channel_id=1, source_target_pairs={{0,16},{2,18},{4,20},{6,22},{8,24},{10,26},{12,28},{14,30},{16,0},... | collective-permute-start | bytes 294920 | tf_op jit(solution)/shard_map/ppermute | solution.py:30
  150.9 11.2 %collective-permute-start.23 = (bf16[32,1536]{1,0:T(8,128)(2,1)S(1)}, bf16[32,1536]{1,0:T(8,128)(2,1)S(1)}, u32[]{:S(2)}, u32[]{:S(2)}) collective-permute-start(bf16[32,1536]{1,0:T(8,128)(2,1)S(1)} %dynamic-slice_bitcast_fusion.8), channel_id=1, source_target_pairs={{0,16},{2,18},{4,20},{6,22},{8,24},{10,26},{12,28},{14,30},{16,0},... | collective-permute-start | bytes 294920 | tf_op jit(solution)/shard_map/ppermute | solution.py:30
  157.9 7.4 %collective-permute-start.15 = (bf16[32,1536]{1,0:T(8,128)(2,1)S(1)}, bf16[32,1536]{1,0:T(8,128)(2,1)S(1)}, u32[]{:S(2)}, u32[]{:S(2)}) collective-permute-start(bf16[32,1536]{1,0:T(8,128)(2,1)S(1)} %fusion.15), channel_id=1, source_target_pairs={{0,16},{2,18},{4,20},{6,22},{8,24},{10,26},{12,28},{14,30},{16,0},... | collective-permute-start | bytes 294920 | tf_op jit(solution)/shard_map/ppermute | solution.py:30
  162.1 5.7 %collective-permute-start.24 = (bf16[32,1536]{1,0:T(8,128)(2,1)S(1)}, bf16[32,1536]{1,0:T(8,128)(2,1)S(1)}, u32[]{:S(2)}, u32[]{:S(2)}) collective-permute-start(bf16[32,1536]{1,0:T(8,128)(2,1)S(1)} %fusion.14), channel_id=1, source_target_pairs={{0,16},{2,18},{4,20},{6,22},{8,24},{10,26},{12,28},{14,30},{16,0},... | collective-permute-start | bytes 294920 | tf_op jit(solution)/shard_map/ppermute | solution.py:30
  165.3 7.3 %collective-permute-start.16 = (bf16[64,1536]{1,0:T(8,128)(2,1)S(1)}, bf16[64,1536]{1,0:T(8,128)(2,1)S(1)}, u32[]{:S(2)}, u32[]{:S(2)}) collective-permute-start(bf16[64,1536]{1,0:T(8,128)(2,1)S(1)} %pad_maximum_fusion.6), channel_id=1, source_target_pairs={{0,8},{2,10},{4,12},{6,14},{8,0},{10,2},{12,4},{14,6},{16,24},{18,... | collective-permute-start | bytes 589832 | tf_op jit(solution)/shard_map/ppermute | solution.py:30
  167.8 6.9 %collective-permute-start.25 = (bf16[64,1536]{1,0:T(8,128)(2,1)S(1)}, bf16[64,1536]{1,0:T(8,128)(2,1)S(1)}, u32[]{:S(2)}, u32[]{:S(2)}) collective-permute-start(bf16[64,1536]{1,0:T(8,128)(2,1)S(1)} %pad_maximum_fusion.7), channel_id=1, source_target_pairs={{0,8},{2,10},{4,12},{6,14},{8,0},{10,2},{12,4},{14,6},{16,24},{18,... | collective-permute-start | bytes 589832 | tf_op jit(solution)/shard_map/ppermute | solution.py:30
  172.7 10.9 %collective-permute-start.17 = (bf16[128,1536]{1,0:T(8,128)(2,1)S(1)}, bf16[128,1536]{1,0:T(8,128)(2,1)S(1)}, u32[]{:S(2)}, u32[]{:S(2)}) collective-permute-start(bf16[128,1536]{1,0:T(8,128)(2,1)S(1)} %pad_maximum_fusion.3), channel_id=1, source_target_pairs={{0,4},{2,6},{4,0},{6,2},{8,12},{10,14},{12,8},{14,10},{16,20},{18,... | collective-permute-start | bytes 1179656 | tf_op jit(solution)/shard_map/ppermute | solution.py:30
  174.8 13.0 %collective-permute-start.26 = (bf16[128,1536]{1,0:T(8,128)(2,1)S(1)}, bf16[128,1536]{1,0:T(8,128)(2,1)S(1)}, u32[]{:S(2)}, u32[]{:S(2)}) collective-permute-start(bf16[128,1536]{1,0:T(8,128)(2,1)S(1)} %pad_maximum_fusion.4), channel_id=1, source_target_pairs={{0,4},{2,6},{4,0},{6,2},{8,12},{10,14},{12,8},{14,10},{16,20},{18,... | collective-permute-start | bytes 1179656 | tf_op jit(solution)/shard_map/ppermute | solution.py:30
  183.8 7.4 %collective-permute-start.18 = (bf16[256,1536]{1,0:T(8,128)(2,1)S(1)}, bf16[256,1536]{1,0:T(8,128)(2,1)S(1)}, u32[]{:S(2)}, u32[]{:S(2)}) collective-permute-start(bf16[256,1536]{1,0:T(8,128)(2,1)S(1)} %pad_maximum_fusion.1.own_0), channel_id=1, source_target_pairs={{0,2},{2,0},{4,6},{6,4},{8,10},{10,8},{12,14},{14,12},{16,18},{18,... | collective-permute-start | bytes 2359304 | tf_op jit(solution)/shard_map/ppermute | solution.py:30
  188.0 3.2 %collective-permute-start.27 = (bf16[256,1536]{1,0:T(8,128)(2,1)S(1)}, bf16[256,1536]{1,0:T(8,128)(2,1)S(1)}, u32[]{:S(2)}, u32[]{:S(2)}) collective-permute-start(bf16[256,1536]{1,0:T(8,128)(2,1)S(1)} %pad_maximum_fusion.2.own_1), channel_id=1, source_target_pairs={{0,2},{2,0},{4,6},{6,4},{8,10},{10,8},{12,14},{14,12},{16,18},{18,... | collective-permute-start | bytes 2359304 | tf_op jit(solution)/shard_map/ppermute | solution.py:30
  (8 other events, 68.1 us)
